TPU v7x, 256 devices: a whole 4x4x8 slice. The times are simulated.
256 devices in a mesh: seq: 32 (over z_hi, x, core), head: 8 (over z_lo, y).
Axes of the slice: x: 4, y: 4, z: 8 (z_hi: 4, z_lo: 2; z = z_hi * 2 + z_lo), core: 2. Of those that a mesh axis runs over, the one named last changes fastest.
Arguments:
- queries: bfloat16 [98304, 4096], P(('seq', 'head')), may hold values from -72 to 72
- key_states: bfloat16 [98304, 4096], P(('seq', 'head')), may hold values from -7 to 7
- value_states: bfloat16 [98304, 4096], P(('seq', 'head')), may hold values from -6 to 6
- partner: int32 [384], replicated, may hold values from 0 to 383, as said below
- buckets: int32 [2, 511], replicated, may hold values from 0 to 31
- bias_table: float32 [32, 32], P(None, 'head'), may hold values from -4 to 4
Outputs:
- attended: bfloat16 [98304, 4096], P(('seq', 'head'))
Inputs may be any that keep to these rules, and one draw needn't show every extreme that they name: `partner`: A permutation of the 384 blocks; block i lies on seq index i // 12. The 12 blocks of one seq index have their partners on 12 different seq indices, and they are the partners of blocks on 12 different seq indices.
All inputs are finite; a program needn't handle non-finite values.
Results may differ from a plain program's by a relative error of at most 0.004.
Values may be sent and summed in bfloat16 or wider, within the bound.
A program may use at most 192 MiB of HBM per device.

v0:
```python
import math

import jax
import jax.numpy as jnp
from jax import lax
from jax.sharding import PartitionSpec as P

BLOCK = 256


def partial_softmax(query_blocks, key_groups, value_groups, bias_groups, score_scale):

    def one_block(items):
        query_one, key_one, value_one = items
        scores = jnp.einsum(
            "qhd,gkhd->ghqk", query_one, key_one, preferred_element_type=jnp.float32
        )
        scores = scores * score_scale + bias_groups
        highest = jnp.max(scores, axis=-1)
        weights = jnp.exp(scores - highest[..., None])
        totals = jnp.sum(weights, axis=-1)
        summed = jnp.einsum(
            "ghqk,gkhd->gqhd",
            weights.astype(jnp.bfloat16),
            value_one,
            preferred_element_type=jnp.float32,
        )
        return (summed, highest, totals)

    summed, highest, totals = lax.map(
        one_block, (query_blocks, jnp.swapaxes(key_groups, 0, 1), jnp.swapaxes(value_groups, 0, 1))
    )
    return (jnp.swapaxes(summed, 0, 1), jnp.swapaxes(highest, 0, 1), jnp.swapaxes(totals, 0, 1))


def combine_parts(first_part, second_part):
    first_sum, first_high, first_total = first_part
    second_sum, second_high, second_total = second_part
    joint_high = jnp.maximum(first_high, second_high)
    first_factor = jnp.exp(first_high - joint_high)
    second_factor = jnp.exp(second_high - joint_high)
    denominator = first_factor * first_total + second_factor * second_total
    numerator = (
        first_sum * jnp.swapaxes(first_factor, 1, 2)[..., None]
        + second_sum * jnp.swapaxes(second_factor, 1, 2)[..., None]
    )
    return (numerator / jnp.swapaxes(denominator, 1, 2)[..., None]).astype(jnp.bfloat16)


def slot_pick(owners, peer_count):
    matches = owners[None, :] == jnp.arange(peer_count, dtype=jnp.int32)[:, None]
    picked = jnp.sum(
        jnp.where(matches, jnp.arange(owners.shape[0], dtype=jnp.int32)[None, :], 0), axis=1
    )
    return (picked, jnp.any(matches, axis=1))


def on_device(queries, key_states, value_states, partner, buckets, bias_table):
    head_queries, head_keys, head_values = (
        lax.all_to_all(queries, "head", split_axis=1, concat_axis=0, tiled=True),
        lax.all_to_all(key_states, "head", split_axis=1, concat_axis=0, tiled=True),
        lax.all_to_all(value_states, "head", split_axis=1, concat_axis=0, tiled=True),
    )
    row_count, column_count = head_queries.shape
    local_heads = bias_table.shape[1]
    head_width = column_count // local_heads
    blocks = row_count // BLOCK
    block_shape = (blocks, BLOCK, local_heads, head_width)
    query_blocks = head_queries.reshape(block_shape)
    key_blocks = head_keys.reshape(block_shape)
    value_blocks = head_values.reshape(block_shape)
    score_scale = 1.0 / math.sqrt(head_width)
    offsets = (
        jnp.arange(BLOCK, dtype=jnp.int32)[None, :]
        - jnp.arange(BLOCK, dtype=jnp.int32)[:, None]
        + (BLOCK - 1)
    )
    bucket_full = jnp.concatenate([buckets[0][offsets], buckets[1][offsets]], axis=1)
    one_hot = (bucket_full[..., None] == jnp.arange(bias_table.shape[0], dtype=jnp.int32)).astype(
        jnp.float32
    )
    bias_all = jnp.einsum("qkb,bh->hqk", one_hot, bias_table, precision=lax.Precision.HIGHEST)
    bias_self = bias_all[:, :, :BLOCK]
    bias_far = bias_all[:, :, BLOCK:]
    peer_count = lax.axis_size("seq")
    first_block = lax.axis_index("seq") * blocks
    my_partners = lax.dynamic_slice_in_dim(partner, first_block, blocks)
    partner_owner = my_partners // blocks
    inverse = jnp.zeros_like(partner).at[partner].set(jnp.arange(partner.shape[0], dtype=jnp.int32))
    asker_owner = lax.dynamic_slice_in_dim(inverse, first_block, blocks) // blocks
    empty_value = jnp.zeros((), jnp.bfloat16)
    picked, occupied = slot_pick(asker_owner, peer_count)
    packed = jnp.concatenate(
        [
            head_keys.reshape(blocks, BLOCK, column_count),
            head_values.reshape(blocks, BLOCK, column_count),
        ],
        axis=-1,
    )
    outgoing = jnp.where(occupied[:, None, None], packed[picked], empty_value)
    arrived = lax.all_to_all(outgoing, "seq", split_axis=0, concat_axis=0, tiled=True)
    chosen = arrived[partner_owner]
    far_keys = chosen[..., :column_count].reshape(block_shape)
    far_values = chosen[..., column_count:].reshape(block_shape)
    joined = partial_softmax(
        query_blocks,
        jnp.stack([key_blocks, far_keys]),
        jnp.stack([value_blocks, far_values]),
        jnp.stack([bias_self, bias_far]),
        score_scale,
    )
    self_parts = tuple((member[0:1] for member in joined))
    far_parts = tuple((member[1:2] for member in joined))
    attended = combine_parts(
        tuple((member[0] for member in self_parts)), tuple((member[0] for member in far_parts))
    )
    return lax.all_to_all(
        attended.reshape(row_count, column_count), "head", split_axis=0, concat_axis=1, tiled=True
    )


def solution(mesh):
    in_specs = (
        P(("seq", "head"), None),
        P(("seq", "head"), None),
        P(("seq", "head"), None),
        P(),
        P(),
        P(None, "head"),
    )
    out_specs = P(("seq", "head"), None)
    return jax.shard_map(
        on_device, mesh=mesh, in_specs=in_specs, out_specs=out_specs, check_vma=False
    )
```

profile of v0, /device:TPU:1, one launch (start us, length us, event | category | flops | bytes accessed | tf_op | source)
XLA Modules:
  0.0 1284.9 jit_solution(15743057259326465030)
XLA Ops:
  4.7 6.4 all-to-all-start.1
  15.7 32.7 %all-to-all-done.1 = bf16[384,8,512]{0,2,1:T(8,128)(2,1)S(1)} async-done(((bf16[384,8,512]{0,2,1:T(8,128)(2,1)}), bf16[384,8,512]{0,2,1:T(8,128)(2,1)S(1)}, u32[]{:S(2)}, u32[]{:S(2)}) %all-to-all-start.1) | async-done | bytes 3145760 | tf_op jit(solution)/shard_map/all_to_all | solution.py:61
  56.8 33.5 %all-to-all-done = bf16[384,8,512]{0,2,1:T(8,128)(2,1)} async-done(((bf16[384,8,512]{0,2,1:T(8,128)(2,1)}), bf16[384,8,512]{0,2,1:T(8,128)(2,1)}, u32[]{:S(2)}, u32[]{:S(2)}) %all-to-all-start) | async-done | bytes 3145760 | tf_op jit(solution)/shard_map/all_to_all | solution.py:62
  101.2 5.4 copy.80
  106.6 5.3 pad_maximum_fusion
  112.0 9.9 gather_fusion
  121.9 14.0 %broadcast_select_fusion = bf16[32,256,1024]{2,1,0:T(8,128)(2,1)} fusion(bf16[32,256,1024]{2,1,0:T(8,128)(2,1)} %gather_fusion, pred[32]{0:T(512)(128)(4,1)S(1)} %fusion.14), kind=kLoop, calls=%fused_computation.21 | loop fusion | flops 8388608 | bytes 33554464 | tf_op jit(solution)/shard_map/jit(_where)/select_n | solution.py:100
  135.8 11.2 all-to-all-start.2
  147.4 407.7 %gather_fusion.2 = s32[65536]{0:T(1024)S(1)} fusion(s32[511]{0:T(512)S(1)} %bitcast.126, s32[65536]{0:T(1024)S(1)} %broadcast_clamp_fusion), kind=kCustom, calls=%fused_computation.2 | custom fusion | bytes 786432 | tf_op jit(solution)/shard_map/gather | solution.py:78
  555.2 407.7 %gather_fusion.3 = s32[65536]{0:T(1024)S(1)} fusion(s32[511]{0:T(512)S(1)} %bitcast.125, s32[65536]{0:T(1024)S(1)} %broadcast_clamp_fusion), kind=kCustom, calls=%fused_computation.3 | custom fusion | bytes 786432 | tf_op jit(solution)/shard_map/gather | solution.py:78
  973.3 5.6 stack_reshape.12
  978.8 5.6 stack_reshape.14
  984.4 5.5 reshape.87
  989.9 10.0 gather_fusion.1
  999.9 6.2 fusion.23
  1010.7 5.9 copy.86
  1016.6 5.5 stack_reshape.13
  1022.1 14.0 %maximum_bitcast_fusion = (bf16[12,2,256,4,128]{4,3,2,0,1:T(4,128)(2,1)}, bf16[12,2,256,4,128]{4,3,2,0,1:T(4,128)(2,1)}) fusion(bf16[1,12,256,4,128]{4,3,2,1,0:T(4,128)(2,1)} %stack_reshape.13, bf16[1,12,256,4,128]{4,3,2,1,0:T(4,128)(2,1)} %stack_reshape.12, bf16[1,12,256,4,128]{4,3,2,1,0:T(4,128)(2,1)} %copy.86, bf16[1,12,256,4,128]{4,3,2,1,0:T(4,128)(2,1)} %stack_reshape.14), kind=kLoop, calls=%fused_computation.25 | loop fusion | flops 6291456 | bytes 25165824 | tf_op jit(solution)/shard_map/transpose | solution.py:31
  1036.1 103.9 %while.14 = (s32[]{:T(128)}, f32[12,2,256,4,128]{2,4,3,1,0:T(8,128)}, f32[12,2,4,256]{3,2,0,1:T(4,128)S(1)}, f32[12,2,4,256]{3,1,2,0:T(2,128)S(1)}, bf16[12,2,25...) while((s32[]{:T(128)}, ...), condition=%wide.region_6.7_spmd, body=%wide.region_3.6_spmd.sunk | while | flops 271577088 | bytes 14475885 | solution.py:30
  1140.0 10.7 fusion.22
  1150.7 7.6 copy.92
  1158.3 7.9 squeeze.37
  1166.2 7.6 copy.95
  1173.7 7.9 squeeze.40
  1182.2 5.4 div.24
  1187.7 7.9 div.25
  1196.1 5.5 mul.40
  1201.5 7.9 mul.41
  1209.9 5.5 mul.43
  1215.4 7.9 mul.44
  1223.3 11.9 divide_convert_fusion
  1235.2 42.2 %all_to_all.69 = bf16[8,384,512]{2,1,0:T(8,128)(2,1)S(1)} all-to-all(bf16[8,384,512]{2,1,0:T(8,128)(2,1)S(1)} %divide_convert_fusion), channel_id=1, replica_groups=mesh['seq'=32,'head'=8] {'head'}, dimensions={0} | all-to-all | bytes 6291456 | tf_op jit(solution)/shard_map/all_to_all | solution.py:117
  (150 shorter events, 156.6 us)
Async XLA Ops:
  0.0 963.0 %copy-start = (f32[32,4]{0,1:T(4,128)S(1)}, f32[32,4]{0,1:T(4,128)}, u32[]{:S(2)}) copy-start(f32[32,4]{0,1:T(4,128)} %param.13) | copy-start | bytes 1540
  4.7 43.8 %all-to-all-start.1 = ((bf16[384,8,512]{0,2,1:T(8,128)(2,1)}), bf16[384,8,512]{0,2,1:T(8,128)(2,1)S(1)}, u32[]{:S(2)}, u32[]{:S(2)}) async-start(bf16[384,8,512]{0,2,1:T(8,128)(2,1)} %bitcast.133), calls=%async_computation.1 | async-start | bytes 6291456 | tf_op jit(solution)/shard_map/all_to_all | solution.py:61
  48.4 8.4 copy-start.2
  48.4 41.8 %all-to-all-start = ((bf16[384,8,512]{0,2,1:T(8,128)(2,1)}), bf16[384,8,512]{0,2,1:T(8,128)(2,1)}, u32[]{:S(2)}, u32[]{:S(2)}) async-start(bf16[384,8,512]{0,2,1:T(8,128)(2,1)} %bitcast.132), calls=%async_computation | async-start | bytes 6291456 | tf_op jit(solution)/shard_map/all_to_all | solution.py:62
  52.9 41.9 %copy-start.6 = (s32[384]{0:T(512)S(1)}, s32[384]{0:T(512)}, u32[]{:S(2)}) copy-start(s32[384]{0:T(512)} %param.11) | copy-start | bytes 4612
  90.3 45.6 %all-to-all-start.3 = ((bf16[384,8,512]{2,0,1:T(8,128)(2,1)}), bf16[384,8,512]{2,0,1:T(8,128)(2,1)}, u32[]{:S(2)}, u32[]{:S(2)}) async-start(bf16[384,8,512]{2,0,1:T(8,128)(2,1)} %bitcast.131), calls=%async_computation.3 | async-start | bytes 6291456 | tf_op jit(solution)/shard_map/all_to_all | solution.py:60
  101.2 10.8 copy-start.1
  135.8 11.5 copy-start.5
  135.8 854.1 %all-to-all-start.2 = ((bf16[32,256,1024]{2,1,0:T(8,128)(2,1)}), bf16[32,256,1024]{2,1,0:T(8,128)(2,1)}, u32[]{:S(2)}, u32[]{:S(2)}) async-start(bf16[32,256,1024]{2,1,0:T(8,128)(2,1)} %broadcast_select_fusion), calls=%async_computation.2 | async-start | bytes 33554432 | tf_op jit(solution)/shard_map/all_to_all | solution.py:101
  1022.1 14.0 %copy-start.3 = (f32[12,2,4,256]{3,1,2,0:T(2,128)S(1)}, f32[12,2,4,256]{3,1,2,0:T(2,128)}, u32[]{:S(2)}) copy-start(f32[12,2,4,256]{3,1,2,0:T(2,128)} %custom-call.10) | copy-start | bytes 294916
  1022.1 14.0 %copy-start.4 = (f32[12,2,4,256]{3,2,0,1:T(4,128)S(1)}, f32[12,2,4,256]{3,2,0,1:T(4,128)}, u32[]{:S(2)}) copy-start(f32[12,2,4,256]{3,2,0,1:T(4,128)} %custom-call.9) | copy-start | bytes 294916
where the time goes:
time: 1290 us; the launch traced here: 1280 us
  local copies, waits for them, and re-layouts  1060 us (82%)
  waiting for transfers between devices  66.2 us (5%)
  other arithmetic  52.4 us (4%)
  blocking collectives  42.2 us (3%)
  matrix products  38.9 us (3%)
  starting transfers between devices  26.5 us (2%)
    gather x2, local copies, waits for them, and re-layouts, on_device(): buckets[0][offsets]  408 us
    gather x2, local copies, waits for them, and re-layouts, on_device(): buckets[1][offsets]  408 us
    dynamic_slice x36, local copies, waits for them, and re-layouts, partial_softmax(): lax.map(one_block, (query_blocks, jnp.swapaxes(key_groups, 0, 1), jnp.swa...  65.8 us
    all_to_all x1, blocking collectives, on_device(): lax.all_to_all(attended.reshape(row_count, column_count), 'head', split_a...  42.2 us
    all_to_all x1, waiting for transfers between devices, on_device(): lax.all_to_all(value_states, 'head', split_axis=1, concat_axis=0, tiled=T...  33.5 us
    all_to_all x1, waiting for transfers between devices, on_device(): lax.all_to_all(key_states, 'head', split_axis=1, concat_axis=0, tiled=True)  32.7 us
    dot_general x12, matrix products, one_block(): jnp.einsum('ghqk,gkhd->gqhd', weights.astype(jnp.bfloat16), value_one, pr...  28.1 us
  transfers between devices with their start and end apart: 4, of which 2 were waited for; matrix products, arithmetic and copies ran while one was open for 69% of the time, Pallas kernels for 0%

commit v1 on v0

v1 whole, which is shorter than its diff:
```python
import functools
import math

import jax
import jax.numpy as jnp
from jax import lax
from jax.experimental import pallas as pl
from jax.experimental.pallas import tpu as pltpu
from jax.sharding import PartitionSpec as P

BLOCK = 256
HALF = 128
HEADS = 32
LANES = 128
ROWS = 16
CHUNKS = 8
GROUP = 4


def pack_kernel(parity_ref, low_ref, high_ref, half_ref, out_ref):
    shift = parity_ref[0] * (HEADS // 2)
    for head in range(HEADS):
        other = (head + HEADS // 2) % HEADS
        out_ref[0, head, 0] = low_ref[:, head * LANES : (head + 1) * LANES]
        out_ref[0, head, 1] = high_ref[:, other * LANES : (other + 1) * LANES]
        moved = lax.rem(head + shift, HEADS)
        out_ref[0, head, 2] = half_ref[:, pl.ds(pl.multiple_of(moved * LANES, LANES), LANES)]


def pack_tiles(parity, states):
    rows, columns = states.shape
    block = (ROWS, columns)
    return pl.pallas_call(
        pack_kernel,
        grid_spec=pltpu.PrefetchScalarGridSpec(
            num_scalar_prefetch=1,
            grid=(CHUNKS,),
            in_specs=[
                pl.BlockSpec(block, lambda c, e: (CHUNKS * e[0] + c, 0)),
                pl.BlockSpec(block, lambda c, e: (CHUNKS * e[0] + CHUNKS + c, 0)),
                pl.BlockSpec(block, lambda c, e: (2 * CHUNKS * (1 - e[0]) + c, 0)),
            ],
            out_specs=pl.BlockSpec((1, HEADS, 3, ROWS, LANES), lambda c, e: (c, 0, 0, 0, 0)),
        ),
        out_shape=jax.ShapeDtypeStruct((CHUNKS, HEADS, 3, ROWS, LANES), states.dtype),
        cost_estimate=pl.CostEstimate(flops=0, transcendentals=0, bytes_accessed=4 * rows * columns),
        name="pack_tiles",
    )(parity, states, states, states)


def pick_kernel(table_ref, held_ref, out_ref):
    count = out_ref.shape[0]
    first = pl.program_id(0) * count

    @pl.loop(0, count, step=16)
    def _(start):
        for offset in range(16):
            out_ref[start + offset] = held_ref[table_ref[first + start + offset]]


def pick_tiles(table, held):
    total = held.shape[0]
    wanted = table.shape[0]
    steps = 4
    return pl.pallas_call(
        pick_kernel,
        grid_spec=pltpu.PrefetchScalarGridSpec(
            num_scalar_prefetch=1,
            grid=(steps,),
            in_specs=[
                pl.BlockSpec((total, ROWS, LANES), lambda i, t: (0, 0, 0)),
            ],
            out_specs=pl.BlockSpec((wanted // steps, ROWS, LANES), lambda i, t: (i, 0, 0)),
        ),
        out_shape=jax.ShapeDtypeStruct((wanted, ROWS, LANES), held.dtype),
        cost_estimate=pl.CostEstimate(flops=0, transcendentals=0, bytes_accessed=16 * 1024 * 1024),
        compiler_params=pltpu.CompilerParams(vmem_limit_bytes=32 * 1024 * 1024),
        name="pick_tiles",
    )(table, held)


def toeplitz_bias(row):
    spread = pltpu.roll(
        jnp.broadcast_to(row, (HALF, 2 * BLOCK)), 2 * BLOCK - HALF + 1, 1, stride=1, stride_axis=0
    )
    return jnp.concatenate([spread[:, HALF : HALF + BLOCK], spread[:, :BLOCK]], axis=0)


def attend_heads(score_scale, query, key, value, far_key, far_value, bias_rows, out_ref):
    for g in range(GROUP):
        columns = slice(g * LANES, (g + 1) * LANES)
        near_keys = key[:, columns]
        near_values = value[:, columns]
        far_keys = jnp.concatenate([half[:, g, 0].reshape(HALF, LANES) for half in far_key], axis=0)
        far_values = jnp.concatenate([half[:, g, 0].reshape(HALF, LANES) for half in far_value], axis=0)
        contract = (((1,), (1,)), ((), ()))
        near = lax.dot_general(
            query[:, columns], near_keys, contract, preferred_element_type=jnp.float32
        )
        far = lax.dot_general(
            query[:, columns], far_keys, contract, preferred_element_type=jnp.float32
        )
        near = near * score_scale + toeplitz_bias(bias_rows[g, 0:1])
        far = far * score_scale + toeplitz_bias(bias_rows[g, 1:2])
        highest = jnp.max(jnp.maximum(near, far), axis=1, keepdims=True)
        near = jnp.exp(near - highest)
        far = jnp.exp(far - highest)
        total = jnp.sum(near + far, axis=1, keepdims=True)
        summed = jnp.dot(
            near.astype(jnp.bfloat16), near_values, preferred_element_type=jnp.float32
        ) + jnp.dot(far.astype(jnp.bfloat16), far_values, preferred_element_type=jnp.float32)
        out_ref[:, columns] = (summed / total).astype(jnp.bfloat16)


def attend_kernel(
    score_scale, parity_ref, q, k, v, ka, kb, va, vb, rows, *rest
):
    out_ref = rest[-1]
    attend_heads(score_scale, q, k, v, (ka, kb), (va, vb), rows, out_ref)


def attend(parity, queries, keys, values, far_keys, key_slot, far_values, value_slot, bias_rows, mode, into):
    width = GROUP * LANES
    steps = HEADS // 2 // GROUP
    score_scale = 1.0 / math.sqrt(LANES)

    def group_of(i, e):
        if mode == "low":
            return i
        if mode == "high":
            return i + steps
        return i + steps * e[0]

    def other_of(i, e):
        if mode == "low":
            return i + steps
        if mode == "high":
            return i
        return i + steps * (1 - e[0])

    if mode == "half":
        local = pl.BlockSpec((BLOCK, width), lambda i, e: (0, i))
        out_shape = jax.ShapeDtypeStruct((BLOCK, steps * width), jnp.bfloat16)
    else:
        local = pl.BlockSpec(
            (pl.Element(BLOCK), pl.Element(width)),
            lambda i, e: (e[0] * HALF, group_of(i, e) * width),
        )
        out_shape = jax.ShapeDtypeStruct(queries.shape, jnp.bfloat16)
    tiles = (CHUNKS, GROUP, 1, ROWS, LANES)
    in_specs = [
        local,
        local,
        local,
        pl.BlockSpec(tiles, lambda i, e: (0, group_of(i, e), key_slot, 0, 0)),
        pl.BlockSpec(tiles, lambda i, e: (0, other_of(i, e), key_slot, 0, 0)),
        pl.BlockSpec(tiles, lambda i, e: (0, group_of(i, e), value_slot, 0, 0)),
        pl.BlockSpec(tiles, lambda i, e: (0, other_of(i, e), value_slot, 0, 0)),
        pl.BlockSpec((GROUP, 2, 2 * BLOCK), lambda i, e: (group_of(i, e), 0, 0)),
    ]
    operands = [parity, queries, keys, values, far_keys, far_keys, far_values, far_values, bias_rows]
    aliases = {}
    if into is not None:
        in_specs.append(pl.BlockSpec(memory_space=pl.ANY))
        aliases = {len(operands): 0}
        operands.append(into)
    return pl.pallas_call(
        functools.partial(attend_kernel, score_scale),
        grid_spec=pltpu.PrefetchScalarGridSpec(
            num_scalar_prefetch=1,
            grid=(steps,),
            in_specs=in_specs,
            out_specs=local,
        ),
        out_shape=out_shape,
        input_output_aliases=aliases,
        cost_estimate=pl.CostEstimate(
            flops=16 * 8 * BLOCK * BLOCK * LANES,
            transcendentals=16 * 2 * BLOCK * BLOCK,
            bytes_accessed=24 * 1024 * 1024,
        ),
        compiler_params=pltpu.CompilerParams(vmem_limit_bytes=40 * 1024 * 1024),
        name="attend_" + mode,
    )(*operands)


def place_kernel(parity_ref, own_ref, other_ref, into_ref, out_ref):
    mine = pl.program_id(0) == parity_ref[0]

    @pl.when(mine)
    def _():
        out_ref[...] = own_ref[...]

    @pl.when(jnp.logical_not(mine))
    def _():
        out_ref[...] = other_ref[...]


def place_half(parity, own, other, into):
    width = own.shape[1]
    return pl.pallas_call(
        place_kernel,
        grid_spec=pltpu.PrefetchScalarGridSpec(
            num_scalar_prefetch=1,
            grid=(2,),
            in_specs=[
                pl.BlockSpec((HALF, width), lambda j, e: (e[0], 0)),
                pl.BlockSpec((HALF, width), lambda j, e: (0, 0)),
                pl.BlockSpec(memory_space=pl.ANY),
            ],
            out_specs=pl.BlockSpec((HALF, width), lambda j, e: (2 * (1 - e[0]), j)),
        ),
        out_shape=jax.ShapeDtypeStruct(into.shape, into.dtype),
        input_output_aliases={3: 0},
        cost_estimate=pl.CostEstimate(flops=0, transcendentals=0, bytes_accessed=4 * HALF * width * 2),
        name="place_half",
    )(parity, own, other, into)


def tile_table(partner, low_side):
    triples = partner.reshape(-1, 3)
    first, middle, last = triples[:, 0], triples[:, 1], triples[:, 2]
    wanted = jnp.stack(
        [
            jnp.stack([first, middle, first], axis=1),
            jnp.stack([last, middle, last], axis=1),
        ],
        axis=1,
    )
    want_low = jnp.array([[True, True, False], [True, False, False]])
    use_first = want_low[None] == low_side
    place = wanted % 3
    head_place = jnp.where(place == 0, 0, jnp.where(place == 1, 2, 3))
    tail_place = jnp.where(place == 0, 1, jnp.where(place == 1, 5, 4))
    return (wanted // 3) * 6 + jnp.where(use_first, head_place, tail_place)


def on_device(queries, key_states, value_states, partner, buckets, bias_table):
    rows, columns = queries.shape
    both = ("seq", "head")
    me = lax.axis_index("seq") * lax.axis_size("head") + lax.axis_index("head")
    devices = lax.axis_size("seq") * lax.axis_size("head")
    odd = lax.rem(me, 2).astype(jnp.int32)
    parity = odd.reshape(1)
    low_side = lax.rem(me, HEADS) < HEADS // 2

    def spread(tiles):
        shape = tiles.shape
        flat = tiles.reshape((devices,) + shape[-3:])
        return lax.all_to_all(flat, both, split_axis=0, concat_axis=0, tiled=True)

    key_tiles = spread(pack_tiles(parity, key_states))
    value_tiles = spread(pack_tiles(parity, value_states))

    swap = [(i, i ^ 1) for i in range(lax.axis_size("head"))]
    half_columns = columns // 2
    half_start = HALF * 2 * (1 - odd)
    halves = jnp.stack(
        [lax.dynamic_slice_in_dim(a, half_start, HALF, 0) for a in (queries, key_states, value_states)]
    )
    kept = lax.dynamic_slice_in_dim(halves, odd * half_columns, half_columns, 2)
    given = lax.dynamic_slice_in_dim(halves, (1 - odd) * half_columns, half_columns, 2)
    taken = lax.ppermute(given, "head", swap)
    is_odd = odd == 1
    middle = jnp.concatenate(
        [jnp.where(is_odd, taken, kept), jnp.where(is_odd, kept, taken)], axis=1
    )

    full_table = lax.all_gather(bias_table, "head", axis=1, tiled=True)
    one_hot = (
        buckets[..., None] == jnp.arange(full_table.shape[0], dtype=jnp.int32)
    ).astype(jnp.float32)
    bias_rows = jnp.einsum("skb,bh->hsk", one_hot, full_table, precision=lax.Precision.HIGHEST)
    bias_rows = jnp.pad(bias_rows, ((0, 0), (0, 0), (0, 1)))

    table = tile_table(partner, low_side)
    tile_shape = (CHUNKS, HEADS, -1, ROWS, LANES)
    far_keys = spread(
        pick_tiles(table.reshape(-1), key_tiles.reshape(-1, ROWS, LANES)).reshape(devices, 3, ROWS, LANES)
    ).reshape(tile_shape)
    flat_values = value_tiles.reshape(-1, ROWS, LANES)
    early_values = spread(
        pick_tiles(table[..., :2].reshape(-1), flat_values).reshape(devices, 2, ROWS, LANES)
    ).reshape(tile_shape)
    late_values = spread(
        pick_tiles(table[..., 2].reshape(-1), flat_values).reshape(devices, 1, ROWS, LANES)
    ).reshape(tile_shape)

    middle_out = attend(
        parity, middle[0], middle[1], middle[2], far_keys, 1, early_values, 1, bias_rows, "half", None
    )
    outgoing = lax.dynamic_slice_in_dim(middle_out, (1 - odd) * HALF, HALF, 0)
    incoming = lax.ppermute(outgoing, "head", swap)
    out = attend(
        parity, queries, key_states, value_states, far_keys, 0, early_values, 0, bias_rows, "low", None
    )
    out = place_half(parity, middle_out, incoming, out)
    return attend(
        parity, queries, key_states, value_states, far_keys, 2, late_values, 0, bias_rows, "high", out
    )


def solution(mesh):
    whole = P(("seq", "head"), None)
    return jax.shard_map(
        on_device,
        mesh=mesh,
        in_specs=(whole, whole, whole, P(), P(), P(None, "head")),
        out_specs=whole,
        check_vma=False,
    )
```

time: 1290 us -> 419 us (0.32)
  local copies, waits for them, and re-layouts: 1060 us -> 24.1 us
  waiting for transfers between devices: 66.2 us -> 250 us
  Pallas kernels: 0 us -> 51.4 us
  other arithmetic: 52.4 us -> 3.69 us
  matrix products: 38.9 us -> 0.2 us
  starting transfers between devices: 26.5 us -> 46.4 us
    gather x6 -> x0, local copies, waits for them, and re-layouts: 835 us -> none  [the longest x2 408 us: on_device(): buckets[0][offsets]]
    all_to_all x4 -> x5, waiting for transfers between devices: 66.2 us -> 250 us  [spread(): return lax.all_to_all(flat, both, split_axis=0, concat_axis=0, tiled=True)]
    dynamic_slice x36 -> x2, local copies, waits for them, and re-layouts: 65.8 us -> 1.37 us  [the longest x1 1.32 us: on_device(): lax.dynamic_slice_in_dim(halves, (1 - odd) * half_columns, half_columns, 2)]
    pallas_call x0 -> x9, Pallas kernels: none -> 51.4 us  [the longest x3 29.9 us: attend(): pl.pallas_call(functools.partial(attend_kernel, score_scale), grid_spec=p...]
    all_to_all x1 -> x0, blocking collectives: 42.2 us -> none  [on_device(): lax.all_to_all(attended.reshape(row_count, column_count), 'head', split_a...]
    all_gather x0 -> x1, blocking collectives: none -> 39.1 us  [on_device(): full_table = lax.all_gather(bias_table, 'head', axis=1, tiled=True)]
    dot_general x25 -> x1, matrix products: 38.9 us -> 0.2 us  [on_device(): jnp.einsum('skb,bh->hsk', one_hot, full_table, precision=lax.Precision.HI...]
    slice x7 -> x10, local copies, waits for them, and re-layouts: 36.8 us -> 0.73 us  [the longest x6 0.45 us: tile_table(): first, middle, last = (triples[:, 0], triples[:, 1], triples[:, 2])]
  transfers between devices with their start and end apart: 4 -> 7, of which waited for: 2 -> 4; matrix products, arithmetic and copies ran while one was open for 69% -> 3% of each run, Pallas kernels for 0% -> 8%
where the time goes in v1:
time: 419 us; the launch traced here: 415 us
  waiting for transfers between devices  250 us (60%)
  Pallas kernels  51.4 us (12%)
  starting transfers between devices  46.4 us (11%)
  blocking collectives  39.1 us (9%)
  local copies, waits for them, and re-layouts  24.1 us (6%)
    all_to_all x5, waiting for transfers between devices, spread(): return lax.all_to_all(flat, both, split_axis=0, concat_axis=0, tiled=True)  250 us
    all_to_all x5, starting transfers between devices, spread(): return lax.all_to_all(flat, both, split_axis=0, concat_axis=0, tiled=True)  44.9 us
    all_gather x1, blocking collectives, on_device(): full_table = lax.all_gather(bias_table, 'head', axis=1, tiled=True)  39.1 us
    pallas_call x3, Pallas kernels, attend(): pl.pallas_call(functools.partial(attend_kernel, score_scale), grid_spec=p...  29.9 us
    unnamed x43, local copies, waits for them, and re-layouts  16 us
    pallas_call x2, Pallas kernels, pack_tiles(): pl.pallas_call(pack_kernel, grid_spec=pltpu.PrefetchScalarGridSpec(num_sc...  13.2 us
  transfers between devices with their start and end apart: 7, of which 4 were waited for; matrix products, arithmetic and copies ran while one was open for 3% of the time, Pallas kernels for 8%

profile of v1, /device:TPU:1, one launch (start us, length us, event | category | flops | bytes accessed | tf_op | source)
XLA Modules:
  0.0 414.9 jit_solution(15273461176776268530)
XLA Ops:
  0.0 6.6 %pack_tiles.3 = bf16[8,32,3,16,128]{4,3,2,1,0:T(8,128)(2,1)} custom-call(s32[1]{0:T(128)} %bitcast.parity_ref, bf16[384,4096]{1,0:T(8,128)(2,1)} %v.3, bf16[384,4096]{1,0:T(8,128)(2,1)} %v.3, bf16[384,4096]{1,0:T(8,128)(2,1)} %v.3), custom_call_target="tpu_custom_call" | custom-call | bytes 6291456 | tf_op jit(solution)/shard_map/pack_tiles/pallas_call | solution.py:33
  6.6 15.7 %all-to-all-start.2 = ((bf16[256,3,16,128]{3,2,1,0:T(8,128)(2,1)}), bf16[256,3,16,128]{3,2,1,0:T(8,128)(2,1)S(1)}, u32[]{:S(2)}, u32[]{:S(2)}) async-start(bf16[256,3,16,128]{3,2,1,0:T(8,128)(2,1)} %bitcast.57), calls=%async_computation.2 | async-start | bytes 6291456 | tf_op jit(solution)/shard_map/all_to_all | solution.py:250
  22.3 6.6 %pack_tiles.2 = bf16[8,32,3,16,128]{4,3,2,1,0:T(8,128)(2,1)} custom-call(s32[1]{0:T(128)} %bitcast.parity_ref, bf16[384,4096]{1,0:T(8,128)(2,1)} %k.3, bf16[384,4096]{1,0:T(8,128)(2,1)} %k.3, bf16[384,4096]{1,0:T(8,128)(2,1)} %k.3), custom_call_target="tpu_custom_call" | custom-call | bytes 6291456 | tf_op jit(solution)/shard_map/pack_tiles/pallas_call | solution.py:33
  28.9 69.2 %all-to-all-done.2 = bf16[256,3,16,128]{3,2,1,0:T(8,128)(2,1)S(1)} async-done(((bf16[256,3,16,128]{3,2,1,0:T(8,128)(2,1)}), bf16[256,3,16,128]{3,2,1,0:T(8,128)(2,1)S(1)}, u32[]{:S(2)}, u32[]{:S(2)}) %all-to-all-start.2) | async-done | bytes 3145760 | tf_op jit(solution)/shard_map/all_to_all | solution.py:250
  98.0 7.9 %all-to-all-start = ((bf16[256,3,16,128]{3,2,1,0:T(8,128)(2,1)}), bf16[256,3,16,128]{3,2,1,0:T(8,128)(2,1)}, u32[]{:S(2)}, u32[]{:S(2)}) async-start(bf16[256,3,16,128]{3,2,1,0:T(8,128)(2,1)} %bitcast.56), calls=%async_computation | async-start | bytes 6291456 | tf_op jit(solution)/shard_map/all_to_all | solution.py:250
  107.2 1.3 pick_tiles.5
  108.5 1.4 copy-done.13
  109.9 71.2 %all-to-all-done = bf16[256,3,16,128]{3,2,1,0:T(8,128)(2,1)} async-done(((bf16[256,3,16,128]{3,2,1,0:T(8,128)(2,1)}), bf16[256,3,16,128]{3,2,1,0:T(8,128)(2,1)}, u32[]{:S(2)}, u32[]{:S(2)}) %all-to-all-start) | async-done | bytes 3145760 | tf_op jit(solution)/shard_map/all_to_all | solution.py:250
  181.1 6.6 %all-to-all-start.4 = ((bf16[256,2,16,128]{3,2,1,0:T(8,128)(2,1)}), bf16[256,2,16,128]{3,2,1,0:T(8,128)(2,1)S(1)}, u32[]{:S(2)}, u32[]{:S(2)}) async-start(bf16[256,2,16,128]{3,2,1,0:T(8,128)(2,1)} %bitcast.54), calls=%async_computation.4 | async-start | bytes 4194304 | tf_op jit(solution)/shard_map/all_to_all | solution.py:250
  189.3 3.6 pick_tiles.3
  192.9 1.7 copy-done.12
  194.6 46.2 %all-to-all-done.4 = bf16[256,2,16,128]{3,2,1,0:T(8,128)(2,1)S(1)} async-done(((bf16[256,2,16,128]{3,2,1,0:T(8,128)(2,1)}), bf16[256,2,16,128]{3,2,1,0:T(8,128)(2,1)S(1)}, u32[]{:S(2)}, u32[]{:S(2)}) %all-to-all-start.4) | async-done | bytes 2097184 | tf_op jit(solution)/shard_map/all_to_all | solution.py:250
  240.8 1.4 copy-done.6
  242.2 6.9 %all-to-all-start.1 = ((bf16[256,3,16,128]{3,2,1,0:T(8,128)(2,1)}), bf16[256,3,16,128]{3,2,1,0:T(8,128)(2,1)S(1)}, u32[]{:S(2)}, u32[]{:S(2)}) async-start(bf16[256,3,16,128]{3,2,1,0:T(8,128)(2,1)} %bitcast.53), calls=%async_computation.1 | async-start | bytes 6291456 | tf_op jit(solution)/shard_map/all_to_all | solution.py:250
  249.1 1.3 dynamic-slice_bitcast_fusion.1
  250.5 1.3 dynamic-slice_bitcast_fusion
  251.8 1.3 dynamic-slice_bitcast_fusion.2
  253.5 1.7 copy-done.16
  255.1 1.3 constant_dynamic-slice_fusion.1
  256.5 1.4 collective-permute-start
  258.1 1.9 copy-done.9
  262.0 62.9 %all-to-all-done.1 = bf16[256,3,16,128]{3,2,1,0:T(8,128)(2,1)S(1)} async-done(((bf16[256,3,16,128]{3,2,1,0:T(8,128)(2,1)}), bf16[256,3,16,128]{3,2,1,0:T(8,128)(2,1)S(1)}, u32[]{:S(2)}, u32[]{:S(2)}) %all-to-all-start.1) | async-done | bytes 3145760 | tf_op jit(solution)/shard_map/all_to_all | solution.py:250
  324.9 7.8 %all-to-all-start.3 = ((bf16[256,1,16,128]{3,2,1,0:T(8,128)(2,1)}), bf16[256,1,16,128]{3,2,1,0:T(8,128)(2,1)}, u32[]{:S(2)}, u32[]{:S(2)}) async-start(bf16[256,1,16,128]{3,2,1,0:T(8,128)(2,1)} %bitcast.55), calls=%async_computation.3 | async-start | bytes 2097152 | tf_op jit(solution)/shard_map/all_to_all | solution.py:250
  332.8 39.1 %all-gather = f32[8,4,32]{2,1,0:T(4,128)S(1)} all-gather(f32[1,4,32]{2,1,0:T(4,128)S(1)} %bitcast.60), channel_id=1, replica_groups=mesh['seq'=32,'head'=8] {'head'}, dimensions={0}, use_global_device_ids=true | all-gather | bytes 4608 | tf_op jit(solution)/shard_map/all_gather | solution.py:269
  372.2 2.8 broadcast_select_fusion
  376.7 9.0 %attend_half.1.own_ref = bf16[256,2048]{1,0:T(8,128)(2,1)S(1)} custom-call(s32[1]{0:T(128)} %bitcast.parity_ref, bf16[256,2048]{1,0:T(8,128)(2,1)S(1)} %get-tuple-element.10.q, bf16[256,2048]{1,0:T(8,128)(2,1)S(1)} %get-tuple-element.11.k, bf16[256,2048]{1,0:T(8,128)(2,1)S(1)} %get-tuple-element.9.v, bf16[8,32,3,16,128]{4,3,2,1,0:T(8,128)(2,1)S(1)} %bitcast.41, ...), custom_call_target="tpu_custom_call" | custom-call | flops 1073741824 | bytes 25165824 | tf_op jit(solution)/shard_map/attend_half/pallas_call | solution.py:167
  385.8 10.5 %attend_low.1.into_ref = bf16[384,4096]{1,0:T(8,128)(2,1)} custom-call(s32[1]{0:T(128)} %bitcast.parity_ref, bf16[384,4096]{1,0:T(8,128)(2,1)S(1)} %copy-done.10, bf16[384,4096]{1,0:T(8,128)(2,1)S(1)} %copy-done.2, bf16[384,4096]{1,0:T(8,128)(2,1)S(1)} %copy-done.4, bf16[8,32,3,16,128]{4,3,2,1,0:T(8,128)(2,1)} %bitcast.43, ...), custom_call_target="tpu_custom_call" | custom-call | flops 1073741824 | bytes 25165824 | tf_op jit(solution)/shard_map/attend_low/pallas_call | solution.py:167
  396.4 2.4 place_half.1.rest_0_
  398.8 1.9 copy-done.3
  400.7 1.9 copy-done.5
  402.6 1.9 copy-done.11
  404.4 10.5 %attend_high.1 = bf16[384,4096]{1,0:T(8,128)(2,1)} custom-call(s32[1]{0:T(128)} %bitcast.parity_ref, bf16[384,4096]{1,0:T(8,128)(2,1)S(1)} %copy-done.11, bf16[384,4096]{1,0:T(8,128)(2,1)S(1)} %copy-done.3, bf16[384,4096]{1,0:T(8,128)(2,1)S(1)} %copy-done.5, bf16[8,32,3,16,128]{4,3,2,1,0:T(8,128)(2,1)S(1)} %bitcast.45, ...), custom_call_target="tpu_custom_call", output_to_operand_aliasing={{}: (9, {})} | custom-call | flops 1073741824 | bytes 25165824 | tf_op jit(solution)/shard_map/attend_high/pallas_call | solution.py:167
  (75 shorter events, 7.3 us)
Async XLA Ops:
  6.6 91.4 %all-to-all-start.2 = ((bf16[256,3,16,128]{3,2,1,0:T(8,128)(2,1)}), bf16[256,3,16,128]{3,2,1,0:T(8,128)(2,1)S(1)}, u32[]{:S(2)}, u32[]{:S(2)}) async-start(bf16[256,3,16,128]{3,2,1,0:T(8,128)(2,1)} %bitcast.57), calls=%async_computation.2 | async-start | bytes 6291456 | tf_op jit(solution)/shard_map/all_to_all | solution.py:250
  98.0 9.1 %copy-start.8 = (bf16[256,3,16,128]{3,2,1,0:T(8,128)(2,1)}, bf16[256,3,16,128]{3,2,1,0:T(8,128)(2,1)S(1)}, u32[]{:S(2)}) copy-start(bf16[256,3,16,128]{3,2,1,0:T(8,128)(2,1)S(1)} %all-to-all-done.2) | copy-start | bytes 9437188
  98.0 7.9 %copy-start.18 = (s32[384]{0:T(512)S(1)}, s32[384]{0:T(512)}, u32[]{:S(2)}) copy-start(s32[384]{0:T(512)} %param.10) | copy-start | bytes 4612
  98.0 8.7 %copy-start.20 = (pred[2,3]{0,1:T(4,128)(4,1)S(1)}, pred[2,3]{0,1:T(4,128)(4,1)}, u32[]{:S(2)}) copy-start(pred[2,3]{0,1:T(4,128)(4,1)} %constant.65.clone) | copy-start | bytes 22
  98.0 83.0 %all-to-all-start = ((bf16[256,3,16,128]{3,2,1,0:T(8,128)(2,1)}), bf16[256,3,16,128]{3,2,1,0:T(8,128)(2,1)}, u32[]{:S(2)}, u32[]{:S(2)}) async-start(bf16[256,3,16,128]{3,2,1,0:T(8,128)(2,1)} %bitcast.56), calls=%async_computation | async-start | bytes 6291456 | tf_op jit(solution)/shard_map/all_to_all | solution.py:250
  108.5 1.4 copy-start.13
  181.1 59.7 %all-to-all-start.4 = ((bf16[256,2,16,128]{3,2,1,0:T(8,128)(2,1)}), bf16[256,2,16,128]{3,2,1,0:T(8,128)(2,1)S(1)}, u32[]{:S(2)}, u32[]{:S(2)}) async-start(bf16[256,2,16,128]{3,2,1,0:T(8,128)(2,1)} %bitcast.54), calls=%async_computation.4 | async-start | bytes 4194304 | tf_op jit(solution)/shard_map/all_to_all | solution.py:250
  192.9 1.7 copy-start.12
  240.8 1.4 copy-start.6
  242.2 82.7 %all-to-all-start.1 = ((bf16[256,3,16,128]{3,2,1,0:T(8,128)(2,1)}), bf16[256,3,16,128]{3,2,1,0:T(8,128)(2,1)S(1)}, u32[]{:S(2)}, u32[]{:S(2)}) async-start(bf16[256,3,16,128]{3,2,1,0:T(8,128)(2,1)} %bitcast.53), calls=%async_computation.1 | async-start | bytes 6291456 | tf_op jit(solution)/shard_map/all_to_all | solution.py:250
  253.5 1.7 copy-start.16
  256.5 115.8 %collective-permute-start = (bf16[3,128,2048]{2,1,0:T(8,128)(2,1)}, bf16[3,128,2048]{2,1,0:T(8,128)(2,1)}, u32[]{:S(2)}, u32[]{:S(2)}) collective-permute-start(bf16[3,128,2048]{2,1,0:T(8,128)(2,1)} %constant_dynamic-slice_fusion.1), channel_id=1, source_target_pairs={{0,1},{1,0},{2,3},{3,2},{4,5},{5,4},{6,7},{7,6},{8,9},{9,8},{10,11... | collective-permute-start | bytes 4718600 | tf_op jit(solution)/shard_map/ppermute | solution.py:263
  258.1 1.9 copy-start.9
  260.0 72.7 %copy-start.19 = (f32[32,4]{0,1:T(4,128)S(1)}, f32[32,4]{0,1:T(4,128)}, u32[]{:S(2)}) copy-start(f32[32,4]{0,1:T(4,128)} %param.12) | copy-start | bytes 1540
  260.0 111.9 %copy-start.17 = (s32[2,511]{1,0:T(2,128)S(1)}, s32[2,511]{1,0:T(2,128)}, u32[]{:S(2)}) copy-start(s32[2,511]{1,0:T(2,128)} %param.11) | copy-start | bytes 12268
  261.0 1.0 copy-start.15
  324.9 50.6 %copy-start = (bf16[256,3,16,128]{3,2,1,0:T(8,128)(2,1)}, bf16[256,3,16,128]{3,2,1,0:T(8,128)(2,1)S(1)}, u32[]{:S(2)}) copy-start(bf16[256,3,16,128]{3,2,1,0:T(8,128)(2,1)S(1)} %all-to-all-done.1) | copy-start | bytes 9437188
  324.9 73.9 %all-to-all-start.3 = ((bf16[256,1,16,128]{3,2,1,0:T(8,128)(2,1)}), bf16[256,1,16,128]{3,2,1,0:T(8,128)(2,1)}, u32[]{:S(2)}, u32[]{:S(2)}) async-start(bf16[256,1,16,128]{3,2,1,0:T(8,128)(2,1)} %bitcast.55), calls=%async_computation.3 | async-start | bytes 2097152 | tf_op jit(solution)/shard_map/all_to_all | solution.py:250
  375.1 1.6 copy-start.7
  376.7 9.2 %copy-start.2 = (bf16[384,4096]{1,0:T(8,128)(2,1)S(1)}, bf16[384,4096]{1,0:T(8,128)(2,1)}, u32[]{:S(2)}) copy-start(bf16[384,4096]{1,0:T(8,128)(2,1)} %k.3) | copy-start | bytes 9437188
  376.7 9.2 %copy-start.4 = (bf16[384,4096]{1,0:T(8,128)(2,1)S(1)}, bf16[384,4096]{1,0:T(8,128)(2,1)}, u32[]{:S(2)}) copy-start(bf16[384,4096]{1,0:T(8,128)(2,1)} %v.3) | copy-start | bytes 9437188
  376.7 9.2 %copy-start.10 = (bf16[384,4096]{1,0:T(8,128)(2,1)S(1)}, bf16[384,4096]{1,0:T(8,128)(2,1)}, u32[]{:S(2)}) copy-start(bf16[384,4096]{1,0:T(8,128)(2,1)} %q.3) | copy-start | bytes 9437188
  385.6 10.7 %copy-start.14 = (bf16[256,2048]{1,0:T(8,128)(2,1)}, bf16[256,2048]{1,0:T(8,128)(2,1)S(1)}, u32[]{:S(2)}) copy-start(bf16[256,2048]{1,0:T(8,128)(2,1)S(1)} %attend_half.1.own_ref) | copy-start | bytes 3145732
  385.7 10.7 %collective-permute-start.1 = (bf16[128,2048]{1,0:T(8,128)(2,1)S(1)}, bf16[128,2048]{1,0:T(8,128)(2,1)}, u32[]{:S(2)}, u32[]{:S(2)}) collective-permute-start(bf16[128,2048]{1,0:T(8,128)(2,1)S(1)} %constant_dynamic-slice_fusion), channel_id=1, source_target_pairs={{0,1},{1,0},{2,3},{3,2},{4,5},{5,4},{6,7},{7,6},{8,9},{9,8},{10,11... | collective-permute-start | bytes 1572872 | tf_op jit(solution)/shard_map/ppermute | solution.py:293
  396.4 2.4 copy-start.1
  398.8 1.9 copy-start.3
  400.7 1.9 copy-start.5
  402.6 1.9 copy-start.11

commit v2 on v1

v2 whole, which is shorter than its diff:
```python
import functools
import math

import jax
import jax.numpy as jnp
from jax import lax
from jax.experimental import pallas as pl
from jax.experimental.pallas import tpu as pltpu
from jax.sharding import PartitionSpec as P

BLOCK = 256
HALF = 128
HEADS = 32
LANES = 128
ROWS = 16
CHUNKS = 8
GROUP = 4


MESH = pl.DeviceIdType.MESH
PLANES = 8
PLANE_DEVICES = 32
SLOTS = 3


def place_of(plane, spot):
    return ((plane // 2) * 8 + spot // 4, lax.rem(plane, 2) * 4 + lax.rem(spot, 4))


def move_kernel(
    table_ref,
    q_ref,
    k_ref,
    v_ref,
    far_ref,
    mid_q_ref,
    mid_k_ref,
    mid_v_ref,
    fanned,
    held_k,
    held_v,
    picked_k,
    picked_v,
    landed,
    half_send,
    half_recv,
    z1_send,
    z1_recv,
    p1_send,
    p1_recv,
    z2_send,
    z2_recv,
    p2_send,
    p2_recv,
):
    seq = lax.axis_index("seq")
    head = lax.axis_index("head")
    plane = 2 * (seq // 8) + head // 4
    spot = lax.rem(seq, 8) * 4 + lax.rem(head, 4)
    odd = lax.rem(head, 2)
    pair = spot + 1 - 2 * odd

    barrier = pltpu.get_barrier_semaphore()
    for step in range(1, PLANES):
        pl.semaphore_signal(
            barrier,
            inc=1,
            device_id=place_of(lax.rem(plane + step, PLANES), spot),
            device_id_type=MESH,
        )

    def greet(step, carry):
        pl.semaphore_signal(
            barrier,
            inc=1,
            device_id=place_of(plane, lax.rem(spot + step, PLANE_DEVICES)),
            device_id_type=MESH,
        )
        return carry

    lax.fori_loop(1, PLANE_DEVICES, greet, 0)
    pl.semaphore_wait(barrier, PLANES - 1 + PLANE_DEVICES - 1)

    def finish(ref, sem):
        pltpu.make_async_copy(ref, ref, sem).wait()

    def z_stage(source, target, send, recv):
        for step in (4, 3, 5, 2, 6, 1, 7):
            other = lax.rem(plane + step, PLANES)
            pltpu.make_async_remote_copy(
                src_ref=source(other),
                dst_ref=target,
                send_sem=send,
                recv_sem=recv,
                device_id=place_of(other, spot),
                device_id_type=MESH,
            ).start()
        pltpu.make_async_copy(source(plane), target, recv).start()

    def plane_stage(source, target, send, recv):
        def body(step, carry):
            other = lax.rem(spot + step, PLANE_DEVICES)
            pltpu.make_async_remote_copy(
                src_ref=source(other),
                dst_ref=target,
                send_sem=send,
                recv_sem=recv,
                device_id=place_of(plane, other),
                device_id_type=MESH,
            ).start()
            return carry

        lax.fori_loop(1, PLANE_DEVICES, body, 0)
        pltpu.make_async_copy(source(spot), target, recv).start()

    def fan_out(chunk):
        kind, slot = divmod(chunk, SLOTS)
        ref = (k_ref, v_ref)[kind]
        first = (odd * HALF, odd * HALF + HALF, 2 * HALF * (1 - odd))[slot]
        z_stage(
            lambda other: ref.at[pl.ds(pl.multiple_of(first + ROWS * other, ROWS), ROWS), :],
            fanned.at[chunk, plane],
            z1_send.at[chunk],
            z1_recv.at[chunk],
        )

    def by_head(chunk):
        kind, slot = divmod(chunk, SLOTS)
        held = (held_k, held_v)[kind]
        shift = (0, HEADS // 2, odd * (HEADS // 2))[slot]

        def source(other):
            start = pl.multiple_of(lax.rem(other + shift, HEADS) * LANES, LANES)
            return fanned.at[chunk, :, :, pl.ds(start, LANES)]

        plane_stage(
            source,
            held.at[pl.ds((slot * PLANE_DEVICES + spot) * PLANES, PLANES)],
            p1_send.at[chunk],
            p1_recv.at[chunk],
        )

    side = spot // (HEADS // 2)
    blocks = table_ref.shape[0] // 2

    def pick(kind, slot):
        held = (held_k, held_v)[kind]
        picked = (picked_k, picked_v)[kind]

        def body(z, carry):
            first = (z // 2) * 96 + lax.rem(z, 2) * 6
            base = (slot * PLANES + z) * PLANE_DEVICES
            for p in range(PLANE_DEVICES):
                e = p % 2
                low = (True, e == 0, False)[slot]
                member = 1 if slot == 1 else 2 * e
                block = first + (p // 4) * 12 + (p % 4 // 2) * 3 + member
                chosen = side if low else 1 - side
                picked[base + p] = held[table_ref[chosen * blocks + block]]
            return carry

        lax.fori_loop(0, PLANES, body, 0)

    def send_picked(chunk):
        kind, slot = divmod(chunk, SLOTS)
        picked = (picked_k, picked_v)[kind]
        z_stage(
            lambda other: picked.at[pl.ds((slot * PLANES + other) * PLANE_DEVICES, PLANE_DEVICES)],
            landed.at[chunk, plane],
            z2_send.at[chunk],
            z2_recv.at[chunk],
        )

    def deliver(chunk):
        plane_stage(
            lambda other: landed.at[chunk, :, other],
            far_ref.at[chunk, spot],
            p2_send.at[chunk],
            p2_recv.at[chunk],
        )

    for chunk in range(SLOTS):
        fan_out(chunk)
    for i, (source, target) in enumerate(((q_ref, mid_q_ref), (k_ref, mid_k_ref), (v_ref, mid_v_ref))):
        rows = pl.ds(pl.multiple_of(2 * HALF * (1 - odd), HALF), HALF)
        width = target.shape[1]
        own = pl.ds(pl.multiple_of(odd * width, LANES), width)
        given = pl.ds(pl.multiple_of((1 - odd) * width, LANES), width)
        place = target.at[pl.ds(pl.multiple_of(odd * HALF, HALF), HALF), :]
        pltpu.make_async_remote_copy(
            src_ref=source.at[rows, given],
            dst_ref=place,
            send_sem=half_send.at[i],
            recv_sem=half_recv.at[i],
            device_id=place_of(plane, pair),
            device_id_type=MESH,
        ).start()
        pltpu.make_async_copy(source.at[rows, own], place, half_recv.at[i]).start()
    for chunk in range(SLOTS):
        finish(fanned.at[chunk], z1_recv.at[chunk])
        by_head(chunk)
        fan_out(chunk + SLOTS)
    for kind in range(2):
        held = (held_k, held_v)[kind]
        for slot in range(SLOTS):
            part = held.at[pl.ds(slot * PLANE_DEVICES * PLANES, PLANE_DEVICES * PLANES)]
            finish(part, p1_recv.at[kind * SLOTS + slot])
        for slot in range(SLOTS):
            pick(kind, slot)
            send_picked(kind * SLOTS + slot)
        if kind == 0:
            for chunk in range(SLOTS, 2 * SLOTS):
                finish(fanned.at[chunk], z1_recv.at[chunk])
                by_head(chunk)
    for chunk in range(2 * SLOTS):
        finish(landed.at[chunk], z2_recv.at[chunk])
        deliver(chunk)
    for i, target in enumerate((mid_q_ref, mid_k_ref, mid_v_ref)):
        finish(target, half_recv.at[i])
        finish(target.at[pl.ds(0, HALF), :], half_send.at[i])
    for chunk in range(2 * SLOTS):
        finish(fanned.at[chunk, pl.ds(0, PLANES - 1)], z1_send.at[chunk])
        finish(far_ref.at[chunk, pl.ds(0, PLANE_DEVICES - 1)], p1_send.at[chunk])
        finish(landed.at[chunk, pl.ds(0, PLANES - 1)], z2_send.at[chunk])
        finish(far_ref.at[chunk, pl.ds(0, PLANE_DEVICES - 1)], p2_send.at[chunk])
    for chunk in range(2 * SLOTS):
        finish(far_ref.at[chunk], p2_recv.at[chunk])


def move_tiles(table, queries, keys, values):
    rows, columns = keys.shape
    kind = keys.dtype
    chunks = 2 * SLOTS
    tiles = SLOTS * PLANES * PLANE_DEVICES
    middle = jax.ShapeDtypeStruct((BLOCK, columns // 2), kind)
    anywhere = pl.BlockSpec(memory_space=pl.ANY)
    semaphores = [pltpu.SemaphoreType.DMA((3,))] * 2 + [pltpu.SemaphoreType.DMA((chunks,))] * 8
    return pl.pallas_call(
        move_kernel,
        in_specs=[pl.BlockSpec(memory_space=pltpu.SMEM)] + [anywhere] * 3,
        out_specs=[anywhere] * 4,
        out_shape=[
            jax.ShapeDtypeStruct((chunks, PLANE_DEVICES, PLANES, ROWS, LANES), kind),
            middle,
            middle,
            middle,
        ],
        scratch_shapes=[
            pltpu.VMEM((chunks, PLANES, ROWS, columns), kind),
            pltpu.VMEM((tiles, ROWS, LANES), kind),
            pltpu.VMEM((tiles, ROWS, LANES), kind),
            pltpu.VMEM((tiles, ROWS, LANES), kind),
            pltpu.VMEM((tiles, ROWS, LANES), kind),
            pltpu.VMEM((chunks, PLANES, PLANE_DEVICES, ROWS, LANES), kind),
        ]
        + semaphores,
        cost_estimate=pl.CostEstimate(
            flops=0, transcendentals=0, bytes_accessed=1024 * 1024 * 1024
        ),
        compiler_params=pltpu.CompilerParams(
            collective_id=0, has_side_effects=True, vmem_limit_bytes=48 * 1024 * 1024
        ),
        name="move_tiles",
    )(table, queries, keys, values)


def toeplitz_bias(row):
    spread = pltpu.roll(
        jnp.broadcast_to(row, (HALF, 2 * BLOCK)), 2 * BLOCK - HALF + 1, 1, stride=1, stride_axis=0
    )
    return jnp.concatenate([spread[:, HALF : HALF + BLOCK], spread[:, :BLOCK]], axis=0)


def attend_heads(score_scale, query, key, value, far_key, far_value, bias_rows, out_ref):
    for g in range(GROUP):
        columns = slice(g * LANES, (g + 1) * LANES)
        near_keys = key[:, columns]
        near_values = value[:, columns]
        far_keys = jnp.concatenate([half[0, g].reshape(HALF, LANES) for half in far_key], axis=0)
        far_values = jnp.concatenate([half[0, g].reshape(HALF, LANES) for half in far_value], axis=0)
        contract = (((1,), (1,)), ((), ()))
        near = lax.dot_general(
            query[:, columns], near_keys, contract, preferred_element_type=jnp.float32
        )
        far = lax.dot_general(
            query[:, columns], far_keys, contract, preferred_element_type=jnp.float32
        )
        near = near * score_scale + toeplitz_bias(bias_rows[g, 0:1])
        far = far * score_scale + toeplitz_bias(bias_rows[g, 1:2])
        highest = jnp.max(jnp.maximum(near, far), axis=1, keepdims=True)
        near = jnp.exp(near - highest)
        far = jnp.exp(far - highest)
        total = jnp.sum(near + far, axis=1, keepdims=True)
        summed = jnp.dot(
            near.astype(jnp.bfloat16), near_values, preferred_element_type=jnp.float32
        ) + jnp.dot(far.astype(jnp.bfloat16), far_values, preferred_element_type=jnp.float32)
        out_ref[:, columns] = (summed / total).astype(jnp.bfloat16)


def attend_kernel(
    score_scale, parity_ref, q, k, v, ka, kb, va, vb, rows, *rest
):
    out_ref = rest[-1]
    attend_heads(score_scale, q, k, v, (ka, kb), (va, vb), rows, out_ref)


def attend(parity, queries, keys, values, far, bias_rows, mode, into):
    slot = {"low": 0, "half": 1, "high": 2}[mode]
    width = GROUP * LANES
    steps = HEADS // 2 // GROUP
    score_scale = 1.0 / math.sqrt(LANES)

    def group_of(i, e):
        if mode == "low":
            return i
        if mode == "high":
            return i + steps
        return i + steps * e[0]

    def other_of(i, e):
        if mode == "low":
            return i + steps
        if mode == "high":
            return i
        return i + steps * (1 - e[0])

    if mode == "half":
        local = pl.BlockSpec((BLOCK, width), lambda i, e: (0, i))
        out_shape = jax.ShapeDtypeStruct((BLOCK, steps * width), jnp.bfloat16)
    else:
        local = pl.BlockSpec(
            (pl.Element(BLOCK), pl.Element(width)),
            lambda i, e: (e[0] * HALF, group_of(i, e) * width),
        )
        out_shape = jax.ShapeDtypeStruct(queries.shape, jnp.bfloat16)
    tiles = (1, GROUP, CHUNKS, ROWS, LANES)
    in_specs = [
        local,
        local,
        local,
        pl.BlockSpec(tiles, lambda i, e: (slot, group_of(i, e), 0, 0, 0)),
        pl.BlockSpec(tiles, lambda i, e: (slot, other_of(i, e), 0, 0, 0)),
        pl.BlockSpec(tiles, lambda i, e: (SLOTS + slot, group_of(i, e), 0, 0, 0)),
        pl.BlockSpec(tiles, lambda i, e: (SLOTS + slot, other_of(i, e), 0, 0, 0)),
        pl.BlockSpec((GROUP, 2, 2 * BLOCK), lambda i, e: (group_of(i, e), 0, 0)),
    ]
    operands = [parity, queries, keys, values, far, far, far, far, bias_rows]
    aliases = {}
    if into is not None:
        in_specs.append(pl.BlockSpec(memory_space=pl.ANY))
        aliases = {len(operands): 0}
        operands.append(into)
    return pl.pallas_call(
        functools.partial(attend_kernel, score_scale),
        grid_spec=pltpu.PrefetchScalarGridSpec(
            num_scalar_prefetch=1,
            grid=(steps,),
            in_specs=in_specs,
            out_specs=local,
        ),
        out_shape=out_shape,
        input_output_aliases=aliases,
        cost_estimate=pl.CostEstimate(
            flops=16 * 8 * BLOCK * BLOCK * LANES,
            transcendentals=16 * 2 * BLOCK * BLOCK,
            bytes_accessed=24 * 1024 * 1024,
        ),
        compiler_params=pltpu.CompilerParams(vmem_limit_bytes=40 * 1024 * 1024),
        name="attend_" + mode,
    )(*operands)


def place_kernel(parity_ref, own_ref, other_ref, into_ref, out_ref):
    mine = pl.program_id(0) == parity_ref[0]

    @pl.when(mine)
    def _():
        out_ref[...] = own_ref[...]

    @pl.when(jnp.logical_not(mine))
    def _():
        out_ref[...] = other_ref[...]


def place_half(parity, own, other, into):
    width = own.shape[1]
    return pl.pallas_call(
        place_kernel,
        grid_spec=pltpu.PrefetchScalarGridSpec(
            num_scalar_prefetch=1,
            grid=(2,),
            in_specs=[
                pl.BlockSpec((HALF, width), lambda j, e: (e[0], 0)),
                pl.BlockSpec((HALF, width), lambda j, e: (0, 0)),
                pl.BlockSpec(memory_space=pl.ANY),
            ],
            out_specs=pl.BlockSpec((HALF, width), lambda j, e: (2 * (1 - e[0]), j)),
        ),
        out_shape=jax.ShapeDtypeStruct(into.shape, into.dtype),
        input_output_aliases={3: 0},
        cost_estimate=pl.CostEstimate(flops=0, transcendentals=0, bytes_accessed=4 * HALF * width * 2),
        name="place_half",
    )(parity, own, other, into)


def tile_table(partner):
    trio = partner // 3
    member = partner - 3 * trio
    entries = []
    for source, slot in (
        (jnp.where(member == 2, 1, 0), jnp.where(member == 1, 2, 0)),
        (jnp.where(member == 0, 0, 1), jnp.where(member == 1, 2, 1)),
    ):
        device = 2 * trio + source
        seq, head = device // 8, device % 8
        plane = (seq // 8) * 2 + head // 4
        spot = (seq % 8) * 4 + head % 4
        entries.append((slot * PLANE_DEVICES + spot) * PLANES + plane)
    return jnp.concatenate(entries)


def on_device(queries, key_states, value_states, partner, buckets, bias_table):
    odd = lax.rem(lax.axis_index("head"), 2).astype(jnp.int32)
    parity = odd.reshape(1)

    full_table = lax.all_gather(bias_table, "head", axis=1, tiled=True)
    one_hot = (
        buckets[..., None] == jnp.arange(full_table.shape[0], dtype=jnp.int32)
    ).astype(jnp.float32)
    bias_rows = jnp.einsum("skb,bh->hsk", one_hot, full_table, precision=lax.Precision.HIGHEST)
    bias_rows = jnp.pad(bias_rows, ((0, 0), (0, 0), (0, 1)))

    far, *middle = move_tiles(tile_table(partner), queries, key_states, value_states)

    middle_out = attend(parity, *middle, far, bias_rows, "half", None)
    outgoing = lax.dynamic_slice_in_dim(middle_out, (1 - odd) * HALF, HALF, 0)
    swap = [(i, i ^ 1) for i in range(lax.axis_size("head"))]
    incoming = lax.ppermute(outgoing, "head", swap)
    out = attend(parity, queries, key_states, value_states, far, bias_rows, "low", None)
    out = attend(parity, queries, key_states, value_states, far, bias_rows, "high", out)
    return place_half(parity, middle_out, incoming, out)


def solution(mesh):
    whole = P(("seq", "head"), None)
    return jax.shard_map(
        on_device,
        mesh=mesh,
        in_specs=(whole, whole, whole, P(), P(), P(None, "head")),
        out_specs=whole,
        check_vma=False,
    )
```

time: 419 us -> 360 us (0.86)
  Pallas kernels: 51.4 us -> 333 us
  waiting for transfers between devices: 250 us -> 0.01 us
  starting transfers between devices: 46.4 us -> 0.77 us
  local copies, waits for them, and re-layouts: 24.1 us -> 3.79 us
  blocking collectives: 39.1 us -> 21 us
    pallas_call x5 -> x1, Pallas kernels: 19.1 us -> 301 us  [move_tiles(): pl.pallas_call(move_kernel, in_specs=[pl.BlockSpec(memory_space=pltpu.SME...]
    all_to_all x5 -> x0, waiting for transfers between devices: 250 us -> none  [spread(): return lax.all_to_all(flat, both, split_axis=0, concat_axis=0, tiled=True)]
    all_to_all x5 -> x0, starting transfers between devices: 44.9 us -> none  [spread(): return lax.all_to_all(flat, both, split_axis=0, concat_axis=0, tiled=True)]
    all_gather x1, blocking collectives: 39.1 us -> 21 us  [on_device(): full_table = lax.all_gather(bias_table, 'head', axis=1, tiled=True)]
    unnamed x43 -> x12, local copies, waits for them, and re-layouts: 16 us -> 3.59 us
  transfers between devices with their start and end apart: 7 -> 1, of which waited for: 4 -> 0; matrix products, arithmetic and copies ran while one was open for 3% -> 0% of each run, Pallas kernels for 8% -> 6%
where the time goes in v2:
time: 360 us
  Pallas kernels  333 us (92%)
  blocking collectives  21 us (6%)
  local copies, waits for them, and re-layouts  3.79 us (1%)
    pallas_call x1, Pallas kernels, move_tiles(): pl.pallas_call(move_kernel, in_specs=[pl.BlockSpec(memory_space=pltpu.SME...  301 us
    pallas_call x3, Pallas kernels, attend(): pl.pallas_call(functools.partial(attend_kernel, score_scale), grid_spec=p...  29.8 us
    all_gather x1, blocking collectives, on_device(): full_table = lax.all_gather(bias_table, 'head', axis=1, tiled=True)  21 us
  transfers between devices with their start and end apart: 1, of which 0 were waited for; matrix products, arithmetic and copies ran while one was open for 0% of the time, Pallas kernels for 6%

profile of v2, /device:TPU:1, one launch (start us, length us, event | category | flops | bytes accessed | tf_op | source)
XLA Modules:
  0.0 360.0 jit_solution(10049449984686454146)
XLA Ops:
  0.0 0.7 fusion.6
  0.7 21.0 %all-gather = f32[8,4,32]{2,1,0:T(4,128)S(1)} all-gather(f32[1,4,32]{2,1,0:T(4,128)} %bitcast.13), channel_id=1, replica_groups=mesh['seq'=32,'head'=8] {'head'}, dimensions={0}, use_global_device_ids=true | all-gather | bytes 4608 | tf_op jit(solution)/shard_map/all_gather | solution.py:426
  21.7 0.9 fusion
  22.6 0.1 copy.12
  22.8 300.7 %move_tiles.1 = (bf16[6,32,8,16,128]{4,3,2,1,0:T(8,128)(2,1)}, bf16[256,2048]{1,0:T(8,128)(2,1)S(1)}, bf16[256,2048]{1,0:T(8,128)(2,1)S(1)}, bf16[256,2048]{1,0:T(8,128)(2,1)S(1)}) custom-call(s32[768]{0:T(1024)S(1)} %pad_add_fusion.table_ref, bf16[384,4096]{1,0:T(8,128)(2,1)} %q.3, bf16[384,4096]{1,0:T(8,128)(2,1)} %k.3, bf16[384,4096]{1,0:T(8,128)(2,1)} %v.3), custom_call_target="tpu_custom_call" | custom-call | bytes 1073741824 | tf_op jit(solution)/shard_map/move_tiles/pallas_call | solution.py:238
  323.5 0.0 copy-start
  323.5 2.8 copy-done
  326.3 0.0 copy-start.1
  326.3 0.0 copy-start.2
  326.3 0.0 copy-start.3
  326.3 8.8 %attend_half.1.own_ref = bf16[256,2048]{1,0:T(8,128)(2,1)S(1)} custom-call(s32[1]{0:T(128)} %bitcast.parity_ref, bf16[256,2048]{1,0:T(8,128)(2,1)S(1)} %get-tuple-element.9.q, bf16[256,2048]{1,0:T(8,128)(2,1)S(1)} %get-tuple-element.10.k, bf16[256,2048]{1,0:T(8,128)(2,1)S(1)} %get-tuple-element.11.v, bf16[6,32,8,16,128]{4,3,2,1,0:T(8,128)(2,1)S(1)} %copy-done, ...), custom_call_target="tpu_custom_call" | custom-call | flops 1073741824 | bytes 25165824 | tf_op jit(solution)/shard_map/attend_half/pallas_call | solution.py:353
  335.1 0.0 copy-start.4
  335.1 0.8 collective-permute-start
  335.9 0.0 copy-done.1
  335.9 0.0 copy-done.2
  335.9 0.0 copy-done.3
  335.9 10.5 %attend_low.1.rest_0_ = bf16[384,4096]{1,0:T(8,128)(2,1)} custom-call(s32[1]{0:T(128)} %bitcast.parity_ref, bf16[384,4096]{1,0:T(8,128)(2,1)S(1)} %copy-done.1, bf16[384,4096]{1,0:T(8,128)(2,1)S(1)} %copy-done.2, bf16[384,4096]{1,0:T(8,128)(2,1)S(1)} %copy-done.3, bf16[6,32,8,16,128]{4,3,2,1,0:T(8,128)(2,1)} %get-tuple-element.12.ka.kb.va.vb, ...), custom_call_target="tpu_custom_call" | custom-call | flops 1073741824 | bytes 25165824 | tf_op jit(solution)/shard_map/attend_low/pallas_call | solution.py:353
  346.5 0.0 copy-done.4
  346.5 10.5 %attend_high.1.into_ref = bf16[384,4096]{1,0:T(8,128)(2,1)} custom-call(s32[1]{0:T(128)} %bitcast.parity_ref, bf16[384,4096]{1,0:T(8,128)(2,1)S(1)} %copy-done.1, bf16[384,4096]{1,0:T(8,128)(2,1)S(1)} %copy-done.2, bf16[384,4096]{1,0:T(8,128)(2,1)S(1)} %copy-done.3, ...), custom_call_target="tpu_custom_call", output_to_operand_aliasing={{}: (9, {})} | custom-call | flops 1073741824 | bytes 25165824 | tf_op jit(solution)/shard_map/attend_high/pallas_call | solution.py:353
  357.0 0.0 collective-permute-done.other_ref
  357.0 0.0 copy-start.5
  357.0 0.8 copy-done.5
  357.8 2.2 place_half.1
  (3 shorter events, 0.1 us)
Async XLA Ops:
  323.5 2.8 copy-start
  326.3 9.6 %copy-start.1 = (bf16[384,4096]{1,0:T(8,128)(2,1)S(1)}, bf16[384,4096]{1,0:T(8,128)(2,1)}, u32[]{:S(2)}) copy-start(bf16[384,4096]{1,0:T(8,128)(2,1)} %q.3) | copy-start | bytes 9437188
  326.3 9.6 %copy-start.2 = (bf16[384,4096]{1,0:T(8,128)(2,1)S(1)}, bf16[384,4096]{1,0:T(8,128)(2,1)}, u32[]{:S(2)}) copy-start(bf16[384,4096]{1,0:T(8,128)(2,1)} %k.3) | copy-start | bytes 9437188
  326.3 9.6 %copy-start.3 = (bf16[384,4096]{1,0:T(8,128)(2,1)S(1)}, bf16[384,4096]{1,0:T(8,128)(2,1)}, u32[]{:S(2)}) copy-start(bf16[384,4096]{1,0:T(8,128)(2,1)} %v.3) | copy-start | bytes 9437188
  335.1 11.4 %copy-start.4 = (bf16[256,2048]{1,0:T(8,128)(2,1)}, bf16[256,2048]{1,0:T(8,128)(2,1)S(1)}, u32[]{:S(2)}) copy-start(bf16[256,2048]{1,0:T(8,128)(2,1)S(1)} %attend_half.1.own_ref) | copy-start | bytes 3145732
  335.1 21.9 %collective-permute-start = (bf16[128,2048]{1,0:T(8,128)(2,1)S(1)}, bf16[128,2048]{1,0:T(8,128)(2,1)S(1)}, u32[]{:S(2)}, u32[]{:S(2)}) collective-permute-start(bf16[128,2048]{1,0:T(8,128)(2,1)S(1)} %constant_dynamic-slice_fusion), channel_id=1, source_target_pairs={{0,1},{1,0},{2,3},{3,2},{4,5},{5,4},{6,7},{7,6},{8,9},{9,8},{10,11... | collective-permute-start | bytes 1572872 | tf_op jit(solution)/shard_map/ppermute | solution.py:438
  357.0 0.8 copy-start.5

commit v3 on v2

v3 whole, which is shorter than its diff:
```python
import math

import jax
import jax.numpy as jnp
from jax import lax
from jax.experimental import pallas as pl
from jax.experimental.pallas import tpu as pltpu
from jax.sharding import PartitionSpec as P

BLOCK = 256
HALF = 128
HEADS = 32
LANES = 128
ROWS = 16
CHUNKS = 8
GROUP = 4


MESH = pl.DeviceIdType.MESH
PLANES = 8
PLANE_DEVICES = 32
SLOTS = 3
ROW_SET = 8


def place_of(plane, spot):
    return ((plane // 2) * 8 + spot // 4, lax.rem(plane, 2) * 4 + lax.rem(spot, 4))


def move_kernel(
    table_ref,
    q_ref,
    k_ref,
    v_ref,
    row_ref,
    far_ref,
    mid_q_ref,
    mid_k_ref,
    mid_v_ref,
    skew_ref,
    fanned,
    held_k,
    held_v,
    picked_k,
    picked_v,
    landed,
    rows,
    skewed,
    row_send,
    row_recv,
    skew_sem,
    half_send,
    half_recv,
    z1_send,
    z1_recv,
    p1_send,
    p1_recv,
    z2_send,
    z2_recv,
    p2_send,
    p2_recv,
):
    seq = lax.axis_index("seq")
    head = lax.axis_index("head")
    plane = 2 * (seq // 8) + head // 4
    spot = lax.rem(seq, 8) * 4 + lax.rem(head, 4)
    odd = lax.rem(head, 2)
    pair = spot + 1 - 2 * odd

    barrier = pltpu.get_barrier_semaphore()
    for step in range(1, PLANES):
        pl.semaphore_signal(
            barrier,
            inc=1,
            device_id=place_of(lax.rem(plane + step, PLANES), spot),
            device_id_type=MESH,
        )

    def greet(step, carry):
        pl.semaphore_signal(
            barrier,
            inc=1,
            device_id=place_of(plane, lax.rem(spot + step, PLANE_DEVICES)),
            device_id_type=MESH,
        )
        return carry

    lax.fori_loop(1, PLANE_DEVICES, greet, 0)
    pl.semaphore_wait(barrier, PLANES - 1 + PLANE_DEVICES - 1)

    def finish(ref, sem):
        pltpu.make_async_copy(ref, ref, sem).wait()

    def z_stage(source, target, send, recv):
        for step in (4, 3, 5, 2, 6, 1, 7):
            other = lax.rem(plane + step, PLANES)
            pltpu.make_async_remote_copy(
                src_ref=source(other),
                dst_ref=target,
                send_sem=send,
                recv_sem=recv,
                device_id=place_of(other, spot),
                device_id_type=MESH,
            ).start()
        pltpu.make_async_copy(source(plane), target, recv).start()

    def plane_stage(source, target, send, recv):
        def body(step, carry):
            other = lax.rem(spot + step, PLANE_DEVICES)
            pltpu.make_async_remote_copy(
                src_ref=source(other),
                dst_ref=target,
                send_sem=send,
                recv_sem=recv,
                device_id=place_of(plane, other),
                device_id_type=MESH,
            ).start()
            return carry

        lax.fori_loop(1, PLANE_DEVICES, body, 0)
        pltpu.make_async_copy(source(spot), target, recv).start()

    def fan_out(chunk):
        kind, slot = divmod(chunk, SLOTS)
        ref = (k_ref, v_ref)[kind]
        first = (odd * HALF, odd * HALF + HALF, 2 * HALF * (1 - odd))[slot]
        z_stage(
            lambda other: ref.at[pl.ds(pl.multiple_of(first + ROWS * other, ROWS), ROWS), :],
            fanned.at[chunk, plane],
            z1_send.at[chunk],
            z1_recv.at[chunk],
        )

    def by_head(chunk):
        kind, slot = divmod(chunk, SLOTS)
        held = (held_k, held_v)[kind]
        shift = (0, HEADS // 2, odd * (HEADS // 2))[slot]

        def source(other):
            start = pl.multiple_of(lax.rem(other + shift, HEADS) * LANES, LANES)
            return fanned.at[chunk, :, :, pl.ds(start, LANES)]

        plane_stage(
            source,
            held.at[pl.ds((slot * PLANE_DEVICES + spot) * PLANES, PLANES)],
            p1_send.at[chunk],
            p1_recv.at[chunk],
        )

    side = spot // (HEADS // 2)
    blocks = table_ref.shape[0] // 2

    def pick(kind, slot):
        held = (held_k, held_v)[kind]
        picked = (picked_k, picked_v)[kind]

        def body(z, carry):
            first = (z // 2) * 96 + lax.rem(z, 2) * 6
            base = (slot * PLANES + z) * PLANE_DEVICES
            for p in range(PLANE_DEVICES):
                e = p % 2
                low = (True, e == 0, False)[slot]
                member = 1 if slot == 1 else 2 * e
                block = first + (p // 4) * 12 + (p % 4 // 2) * 3 + member
                chosen = side if low else 1 - side
                picked[base + p] = held[table_ref[chosen * blocks + block]]
            return carry

        lax.fori_loop(0, PLANES, body, 0)

    def send_picked(chunk):
        kind, slot = divmod(chunk, SLOTS)
        picked = (picked_k, picked_v)[kind]
        z_stage(
            lambda other: picked.at[pl.ds((slot * PLANES + other) * PLANE_DEVICES, PLANE_DEVICES)],
            landed.at[chunk, plane],
            z2_send.at[chunk],
            z2_recv.at[chunk],
        )

    def deliver(chunk):
        plane_stage(
            lambda other: landed.at[chunk, :, other],
            far_ref.at[chunk, spot],
            p2_send.at[chunk],
            p2_recv.at[chunk],
        )

    lower = lax.rem(plane, 2)
    set_rows = 4 * ROW_SET
    near_rows = rows.at[pl.ds(pl.multiple_of(lower * set_rows, ROW_SET), set_rows)]
    far_rows = rows.at[pl.ds(pl.multiple_of((1 - lower) * set_rows, ROW_SET), set_rows)]
    own_rows = rows.at[pl.ds(pl.multiple_of(head * ROW_SET, ROW_SET), ROW_SET)]

    for step in range(1, 4):
        other = spot - lax.rem(spot, 4) + lax.rem(spot + step, 4)
        pltpu.make_async_remote_copy(
            src_ref=row_ref,
            dst_ref=own_rows,
            send_sem=row_send.at[0],
            recv_sem=row_recv.at[0],
            device_id=place_of(plane, other),
            device_id_type=MESH,
        ).start()
    pltpu.make_async_copy(row_ref, own_rows, row_recv.at[0]).start()

    def share_rows():
        finish(near_rows, row_recv.at[0])
        pltpu.make_async_remote_copy(
            src_ref=near_rows,
            dst_ref=near_rows,
            send_sem=row_send.at[1],
            recv_sem=row_recv.at[1],
            device_id=place_of(plane + 1 - 2 * lower, spot),
            device_id_type=MESH,
        ).start()

    def skew_rows():
        finish(far_rows, row_recv.at[1])

        def body(i, carry):
            start = pl.multiple_of(i * ROW_SET, ROW_SET)
            some = rows[pl.ds(start, ROW_SET), :]
            for j in range(ROW_SET):
                turned = pltpu.roll(
                    jnp.broadcast_to(some[j : j + 1], (HALF, 2 * BLOCK)),
                    2 * BLOCK - HALF + 1,
                    1,
                    stride=1,
                    stride_axis=0,
                )
                skewed[start + j] = turned[:, : BLOCK + HALF]
            return carry

        lax.fori_loop(0, 2 * HEADS // ROW_SET, body, 0)
        pltpu.make_async_copy(skewed, skew_ref, skew_sem).start()

    for chunk in range(SLOTS):
        fan_out(chunk)
    for i, (source, target) in enumerate(((q_ref, mid_q_ref), (k_ref, mid_k_ref), (v_ref, mid_v_ref))):
        half_rows = pl.ds(pl.multiple_of(2 * HALF * (1 - odd), HALF), HALF)
        width = target.shape[1]
        own = pl.ds(pl.multiple_of(odd * width, LANES), width)
        given = pl.ds(pl.multiple_of((1 - odd) * width, LANES), width)
        place = target.at[pl.ds(pl.multiple_of(odd * HALF, HALF), HALF), :]
        pltpu.make_async_remote_copy(
            src_ref=source.at[half_rows, given],
            dst_ref=place,
            send_sem=half_send.at[i],
            recv_sem=half_recv.at[i],
            device_id=place_of(plane, pair),
            device_id_type=MESH,
        ).start()
        pltpu.make_async_copy(source.at[half_rows, own], place, half_recv.at[i]).start()
    for chunk in range(SLOTS):
        finish(fanned.at[chunk], z1_recv.at[chunk])
        by_head(chunk)
        fan_out(chunk + SLOTS)
    for kind in range(2):
        held = (held_k, held_v)[kind]
        for slot in range(SLOTS):
            part = held.at[pl.ds(slot * PLANE_DEVICES * PLANES, PLANE_DEVICES * PLANES)]
            finish(part, p1_recv.at[kind * SLOTS + slot])
        for slot in range(SLOTS):
            pick(kind, slot)
            send_picked(kind * SLOTS + slot)
        if kind == 0:
            share_rows()
            for chunk in range(SLOTS, 2 * SLOTS):
                finish(fanned.at[chunk], z1_recv.at[chunk])
                by_head(chunk)
            skew_rows()
    for chunk in range(2 * SLOTS):
        finish(landed.at[chunk], z2_recv.at[chunk])
        deliver(chunk)
    for i, target in enumerate((mid_q_ref, mid_k_ref, mid_v_ref)):
        finish(target, half_recv.at[i])
        finish(target.at[pl.ds(0, HALF), :], half_send.at[i])
    for chunk in range(2 * SLOTS):
        finish(fanned.at[chunk, pl.ds(0, PLANES - 1)], z1_send.at[chunk])
        finish(far_ref.at[chunk, pl.ds(0, PLANE_DEVICES - 1)], p1_send.at[chunk])
        finish(landed.at[chunk, pl.ds(0, PLANES - 1)], z2_send.at[chunk])
        finish(far_ref.at[chunk, pl.ds(0, PLANE_DEVICES - 1)], p2_send.at[chunk])
    finish(rows.at[pl.ds(0, 3 * ROW_SET)], row_send.at[0])
    finish(near_rows, row_send.at[1])
    finish(skew_ref, skew_sem)
    for chunk in range(2 * SLOTS):
        finish(far_ref.at[chunk], p2_recv.at[chunk])


def move_tiles(table, queries, keys, values, own_rows):
    rows, columns = keys.shape
    kind = keys.dtype
    chunks = 2 * SLOTS
    tiles = SLOTS * PLANES * PLANE_DEVICES
    middle = jax.ShapeDtypeStruct((BLOCK, columns // 2), kind)
    anywhere = pl.BlockSpec(memory_space=pltpu.HBM)
    semaphores = [pltpu.SemaphoreType.DMA((2,))] * 2 + [pltpu.SemaphoreType.DMA]
    semaphores += [pltpu.SemaphoreType.DMA((3,))] * 2 + [pltpu.SemaphoreType.DMA((chunks,))] * 8
    return pl.pallas_call(
        move_kernel,
        in_specs=[pl.BlockSpec(memory_space=pltpu.SMEM)]
        + [anywhere] * 3
        + [pl.BlockSpec(memory_space=pltpu.VMEM)],
        out_specs=[anywhere] * 5,
        out_shape=[
            jax.ShapeDtypeStruct((chunks, PLANE_DEVICES, PLANES, ROWS, LANES), kind),
            middle,
            middle,
            middle,
            jax.ShapeDtypeStruct((2 * HEADS, HALF, BLOCK + HALF), jnp.float32),
        ],
        scratch_shapes=[
            pltpu.VMEM((chunks, PLANES, ROWS, columns), kind),
            pltpu.VMEM((tiles, ROWS, LANES), kind),
            pltpu.VMEM((tiles, ROWS, LANES), kind),
            pltpu.VMEM((tiles, ROWS, LANES), kind),
            pltpu.VMEM((tiles, ROWS, LANES), kind),
            pltpu.VMEM((chunks, PLANES, PLANE_DEVICES, ROWS, LANES), kind),
            pltpu.VMEM((2 * HEADS, 2 * BLOCK), jnp.float32),
            pltpu.VMEM((2 * HEADS, HALF, BLOCK + HALF), jnp.float32),
        ]
        + semaphores,
        cost_estimate=pl.CostEstimate(
            flops=0, transcendentals=0, bytes_accessed=1024 * 1024 * 1024
        ),
        compiler_params=pltpu.CompilerParams(
            collective_id=0, has_side_effects=True, vmem_limit_bytes=48 * 1024 * 1024
        ),
        name="move_tiles",
    )(table, queries, keys, values, own_rows)


def attend_kernel(parity_ref, q, k, v, ka, kb, va, vb, skew, out_ref):
    scale = math.log2(math.e) / math.sqrt(LANES)
    contract = (((1,), (1,)), ((), ()))
    ones = jnp.ones((BLOCK, LANES), jnp.bfloat16)
    for g in range(GROUP):
        columns = slice(g * LANES, (g + 1) * LANES)
        near_keys = k[:, columns]
        far_keys = jnp.concatenate([half[0, g].reshape(HALF, LANES) for half in (ka, kb)], axis=0)
        far_values = jnp.concatenate([half[0, g].reshape(HALF, LANES) for half in (va, vb)], axis=0)
        near_values = jnp.concatenate([v[:, columns], ones], axis=1)
        far_values = jnp.concatenate([far_values, ones], axis=1)
        for half in range(2):
            shift = HALF * (1 - half)
            rows = slice(half * HALF, (half + 1) * HALF)
            query = q[rows, columns]
            near = lax.dot_general(query, near_keys, contract, preferred_element_type=jnp.float32)
            far = lax.dot_general(query, far_keys, contract, preferred_element_type=jnp.float32)
            near = near * scale + skew[2 * g, :, shift : shift + BLOCK]
            far = far * scale + skew[2 * g + 1, :, shift : shift + BLOCK]
            highest = jnp.max(jnp.maximum(near, far), axis=1, keepdims=True)
            near = jnp.exp2(near - highest).astype(jnp.bfloat16)
            far = jnp.exp2(far - highest).astype(jnp.bfloat16)
            summed = jnp.dot(near, near_values, preferred_element_type=jnp.float32) + jnp.dot(
                far, far_values, preferred_element_type=jnp.float32
            )
            out_ref[rows, columns] = (summed[:, :LANES] / summed[:, LANES:]).astype(jnp.bfloat16)


def attend(parity, queries, keys, values, far, skewed, middle):
    width = GROUP * LANES
    half_steps = HEADS // 2 // GROUP
    steps = half_steps if middle else 2 * half_steps

    def group_of(i, e):
        return i + half_steps * e[0] if middle else i

    def other_of(i, e):
        return lax.rem(group_of(i, e) + half_steps, 2 * half_steps)

    def slot_of(i):
        return 1 if middle else 2 * (i // half_steps)

    if middle:
        local = pl.BlockSpec((BLOCK, width), lambda i, e: (0, i))
    else:
        local = pl.BlockSpec(
            (pl.Element(BLOCK), pl.Element(width)), lambda i, e: (e[0] * HALF, i * width)
        )
    tiles = (1, GROUP, CHUNKS, ROWS, LANES)
    return pl.pallas_call(
        attend_kernel,
        grid_spec=pltpu.PrefetchScalarGridSpec(
            num_scalar_prefetch=1,
            grid=(steps,),
            in_specs=[
                local,
                local,
                local,
                pl.BlockSpec(tiles, lambda i, e: (slot_of(i), group_of(i, e), 0, 0, 0)),
                pl.BlockSpec(tiles, lambda i, e: (slot_of(i), other_of(i, e), 0, 0, 0)),
                pl.BlockSpec(tiles, lambda i, e: (SLOTS + slot_of(i), group_of(i, e), 0, 0, 0)),
                pl.BlockSpec(tiles, lambda i, e: (SLOTS + slot_of(i), other_of(i, e), 0, 0, 0)),
                pl.BlockSpec(
                    (2 * GROUP, HALF, BLOCK + HALF), lambda i, e: (group_of(i, e), 0, 0)
                ),
            ],
            out_specs=local,
        ),
        out_shape=jax.ShapeDtypeStruct(queries.shape, jnp.bfloat16),
        cost_estimate=pl.CostEstimate(
            flops=steps * GROUP * 8 * BLOCK * BLOCK * LANES,
            transcendentals=steps * GROUP * 2 * BLOCK * BLOCK,
            bytes_accessed=steps * 4 * 1024 * 1024,
        ),
        compiler_params=pltpu.CompilerParams(vmem_limit_bytes=60 * 1024 * 1024),
        name="attend_middle" if middle else "attend_whole",
    )(parity, queries, keys, values, far, far, far, far, skewed)


def place_kernel(parity_ref, own_ref, other_ref, into_ref, out_ref, sems):
    odd = parity_ref[0]
    width = own_ref.shape[1]
    rows = pl.ds(pl.multiple_of(2 * HALF * (1 - odd), HALF), HALF)
    own = pltpu.make_async_copy(
        own_ref.at[pl.ds(pl.multiple_of(odd * HALF, HALF), HALF), :],
        out_ref.at[rows, pl.ds(pl.multiple_of(odd * width, LANES), width)],
        sems.at[0],
    )
    other = pltpu.make_async_copy(
        other_ref,
        out_ref.at[rows, pl.ds(pl.multiple_of((1 - odd) * width, LANES), width)],
        sems.at[1],
    )
    own.start()
    other.start()
    own.wait()
    other.wait()


def place_half(parity, own, other, into):
    anywhere = pl.BlockSpec(memory_space=pltpu.HBM)
    return pl.pallas_call(
        place_kernel,
        in_specs=[pl.BlockSpec(memory_space=pltpu.SMEM)] + [anywhere] * 3,
        out_specs=anywhere,
        out_shape=jax.ShapeDtypeStruct(into.shape, into.dtype),
        scratch_shapes=[pltpu.SemaphoreType.DMA((2,))],
        input_output_aliases={3: 0},
        cost_estimate=pl.CostEstimate(
            flops=0, transcendentals=0, bytes_accessed=4 * HALF * own.shape[1] * 2
        ),
        compiler_params=pltpu.CompilerParams(vmem_limit_bytes=60 * 1024 * 1024),
        name="place_half",
    )(parity, own, other, into)


def tile_table(partner):
    trio = partner // 3
    member = partner - 3 * trio
    entries = []
    for source, slot in (
        (jnp.where(member == 2, 1, 0), jnp.where(member == 1, 2, 0)),
        (jnp.where(member == 0, 0, 1), jnp.where(member == 1, 2, 1)),
    ):
        device = 2 * trio + source
        seq, head = device // 8, device % 8
        plane = (seq // 8) * 2 + head // 4
        spot = (seq % 8) * 4 + head % 4
        entries.append((slot * PLANE_DEVICES + spot) * PLANES + plane)
    return jnp.concatenate(entries)


def on_device(queries, key_states, value_states, partner, buckets, bias_table):
    odd = lax.rem(lax.axis_index("head"), 2).astype(jnp.int32)
    parity = odd.reshape(1)

    one_hot = (
        buckets[..., None] == jnp.arange(bias_table.shape[0], dtype=jnp.int32)
    ).astype(jnp.float32)
    own_rows = jnp.einsum("skb,bh->hsk", one_hot, bias_table, precision=lax.Precision.HIGHEST)
    own_rows = jnp.pad(own_rows * math.log2(math.e), ((0, 0), (0, 0), (0, 1)))

    far, mid_q, mid_k, mid_v, skewed = move_tiles(
        tile_table(partner), queries, key_states, value_states, own_rows.reshape(ROW_SET, 2 * BLOCK)
    )
    middle = attend(parity, mid_q, mid_k, mid_v, far, skewed, True)
    outgoing = lax.dynamic_slice_in_dim(middle, (1 - odd) * HALF, HALF, 0)
    swap = [(i, i ^ 1) for i in range(lax.axis_size("head"))]
    incoming = lax.ppermute(outgoing, "head", swap)
    out = attend(parity, queries, key_states, value_states, far, skewed, False)
    return place_half(parity, middle, incoming, out)


def solution(mesh):
    whole = P(("seq", "head"), None)
    return jax.shard_map(
        on_device,
        mesh=mesh,
        in_specs=(whole, whole, whole, P(), P(), P(None, "head")),
        out_specs=whole,
        check_vma=False,
    )
```

time: 360 us -> 369 us (1.025)
  Pallas kernels: 333 us -> 361 us
  blocking collectives: 21 us -> 0 us
    pallas_call x4 -> x3, Pallas kernels: 32 us -> 54.3 us  [the longest x1 32.9 us: place_half(): pl.pallas_call(place_kernel, in_specs=[pl.BlockSpec(memory_space=pltpu.SM...]
    all_gather x1 -> x0, blocking collectives: 21 us -> none  [on_device(): full_table = lax.all_gather(bias_table, 'head', axis=1, tiled=True)]
    pallas_call x1, Pallas kernels: 301 us -> 307 us  [move_tiles(): pl.pallas_call(move_kernel, in_specs=[pl.BlockSpec(memory_space=pltpu.SME...]
  transfers between devices with their start and end apart: 1 -> 1, of which waited for: 0 -> 0; matrix products, arithmetic and copies ran while one was open for 0% -> 0% of each run, Pallas kernels for 6% -> 4%
where the time goes in v3:
time: 369 us; the launch traced here: 368 us
  Pallas kernels  361 us (98%)
  local copies, waits for them, and re-layouts  4.82 us (1%)
    pallas_call x1, Pallas kernels, move_tiles(): pl.pallas_call(move_kernel, in_specs=[pl.BlockSpec(memory_space=pltpu.SME...  307 us
    pallas_call x1, Pallas kernels, place_half(): pl.pallas_call(place_kernel, in_specs=[pl.BlockSpec(memory_space=pltpu.SM...  32.9 us
    pallas_call x2, Pallas kernels, attend(): pl.pallas_call(attend_kernel, grid_spec=pltpu.PrefetchScalarGridSpec(num_...  21.4 us
  transfers between devices with their start and end apart: 1, of which 0 were waited for; matrix products, arithmetic and copies ran while one was open for 0% of the time, Pallas kernels for 4%

profile of v3, /device:TPU:1, one launch (start us, length us, event | category | flops | bytes accessed | tf_op | source)
XLA Modules:
  0.0 367.9 jit_solution(2460229289074708763)
XLA Ops:
  0.0 0.0 copy-start
  0.0 0.7 fusion.6
  0.7 0.0 copy-done
  0.8 0.8 fusion
  1.7 306.9 %move_tiles.1 = (bf16[6,32,8,16,128]{4,3,2,1,0:T(8,128)(2,1)}, bf16[256,2048]{1,0:T(8,128)(2,1)S(1)}, bf16[256,2048]{1,0:T(8,128)(2,1)S(1)}, bf16[256,2048]{1,0:T(8,128)(2,1)S(1)}, f32[64,128,384]{2,1,0:T(8,128)}) custom-call(s32[768]{0:T(1024)S(1)} %pad_add_fusion.table_ref, bf16[384,4096]{1,0:T(8,128)(2,1)} %q.1, bf16[384,4096]{1,0:T(8,128)(2,1)} %k.1, ...), custom_call_target="tpu_custom_call" | custom-call | bytes 1073741824 | tf_op jit(solution)/shard_map/move_tiles/pallas_call | solution.py:300
  308.5 0.0 copy-start.1
  308.6 1.0 copy-done.1
  309.5 0.0 copy-start.2
  309.5 1.0 copy-done.2
  310.5 0.0 copy-start.3
  310.5 1.0 copy-done.3
  311.5 7.7 %attend_middle.1.own_ref = bf16[256,2048]{1,0:T(8,128)(2,1)} custom-call(s32[1]{0:T(128)} %bitcast.parity_ref, bf16[256,2048]{1,0:T(8,128)(2,1)} %copy-done.1, bf16[256,2048]{1,0:T(8,128)(2,1)} %copy-done.2, bf16[256,2048]{1,0:T(8,128)(2,1)} %copy-done.3, bf16[6,32,8,16,128]{4,3,2,1,0:T(8,128)(2,1)} %get-tuple-element.13.ka.kb.va.vb, ...), custom_call_target="tpu_custom_call" | custom-call | flops 1073741824 | bytes 16777216 | tf_op jit(solution)/shard_map/attend_middle/pallas_call | solution.py:383
  319.2 1.1 constant_dynamic-slice_fusion
  320.3 0.2 collective-permute-start
  320.5 13.7 %attend_whole.1.into_ref = bf16[384,4096]{1,0:T(8,128)(2,1)} custom-call(s32[1]{0:T(128)} %bitcast.parity_ref, bf16[384,4096]{1,0:T(8,128)(2,1)} %q.1, bf16[384,4096]{1,0:T(8,128)(2,1)} %k.1, bf16[384,4096]{1,0:T(8,128)(2,1)} %v.1, bf16[6,32,8,16,128]{4,3,2,1,0:T(8,128)(2,1)} %get-tuple-element.13.ka.kb.va.vb, ...), custom_call_target="tpu_custom_call" | custom-call | flops 2147483648 | bytes 33554432 | tf_op jit(solution)/shard_map/attend_whole/pallas_call | solution.py:383
  334.2 0.0 collective-permute-done.other_ref
  334.2 0.0 copy-start.4
  334.2 0.8 copy-done.4
  335.0 32.9 %place_half.1 = bf16[384,4096]{1,0:T(8,128)(2,1)} custom-call(s32[1]{0:T(128)} %bitcast.parity_ref, bf16[256,2048]{1,0:T(8,128)(2,1)} %attend_middle.1.own_ref, bf16[128,2048]{1,0:T(8,128)(2,1)} %copy-done.4, bf16[384,4096]{1,0:T(8,128)(2,1)} %attend_whole.1.into_ref), custom_call_target="tpu_custom_call", output_to_operand_aliasing={{}: (3, {})} | custom-call | bytes 2097152 | tf_op jit(solution)/shard_map/place_half/pallas_call | solution.py:435
  (4 shorter events, 0.0 us)
Async XLA Ops:
  0.0 0.7 copy-start
  308.5 1.0 copy-start.1
  309.5 1.0 copy-start.2
  310.5 1.0 copy-start.3
  320.3 13.9 %collective-permute-start = (bf16[128,2048]{1,0:T(8,128)(2,1)S(1)}, bf16[128,2048]{1,0:T(8,128)(2,1)S(1)}, u32[]{:S(2)}, u32[]{:S(2)}) collective-permute-start(bf16[128,2048]{1,0:T(8,128)(2,1)S(1)} %constant_dynamic-slice_fusion), channel_id=1, source_target_pairs={{0,1},{1,0},{2,3},{3,2},{4,5},{5,4},{6,7},{7,6},{8,9},{9,8},{10,11... | collective-permute-start | bytes 1572872 | tf_op jit(solution)/shard_map/ppermute | solution.py:482
  334.2 0.8 copy-start.4

commit v4 on v3

--- a/solution.py
+++ b/solution.py
@@ -33,11 +33,16 @@
     k_ref,
     v_ref,
     row_ref,
+    out_ref,
     far_ref,
     mid_q_ref,
     mid_k_ref,
     mid_v_ref,
-    skew_ref,
+    whole_q,
+    whole_k,
+    whole_v,
+    whole_out,
+    middle_out,
     fanned,
     held_k,
     held_v,
@@ -48,7 +53,10 @@
     skewed,
     row_send,
     row_recv,
-    skew_sem,
+    whole_sem,
+    out_sem,
+    swap_send,
+    swap_recv,
     half_send,
     half_recv,
     z1_send,
@@ -233,7 +241,84 @@
             return carry
 
         lax.fori_loop(0, 2 * HEADS // ROW_SET, body, 0)
-        pltpu.make_async_copy(skewed, skew_ref, skew_sem).start()
+
+    scale = math.log2(math.e) / math.sqrt(LANES)
+    contract = (((1,), (1,)), ((), ()))
+    half_heads = HEADS // 2
+
+    def attend(slot):
+        middle = slot == 1
+        first = (0, half_heads * odd, half_heads)[slot]
+        q, k, v = (mid_q_ref, mid_k_ref, mid_v_ref) if middle else (whole_q, whole_k, whole_v)
+        target = middle_out if middle else whole_out
+        ones = jnp.ones((BLOCK, LANES), jnp.bfloat16)
+
+        def body(i, carry):
+            for g in range(GROUP):
+                head = first + i * GROUP + g
+                other = lax.rem(head + half_heads, HEADS)
+                start = (i * GROUP + g if middle else head) * LANES
+                columns = pl.ds(pl.multiple_of(start, LANES), LANES)
+                near_keys = k[:, columns]
+                near_values = jnp.concatenate([v[:, columns], ones], axis=1)
+                far_keys, far_values = (
+                    jnp.concatenate(
+                        [far_ref[chunk, one].reshape(HALF, LANES) for one in (head, other)], axis=0
+                    )
+                    for chunk in (slot, SLOTS + slot)
+                )
+                far_values = jnp.concatenate([far_values, ones], axis=1)
+                for half in range(2):
+                    shift = HALF * (1 - half)
+                    rows_here = slice(half * HALF, (half + 1) * HALF)
+                    query = q[rows_here, columns]
+                    near = lax.dot_general(
+                        query, near_keys, contract, preferred_element_type=jnp.float32
+                    )
+                    far = lax.dot_general(
+                        query, far_keys, contract, preferred_element_type=jnp.float32
+                    )
+                    near = near * scale + skewed[2 * head, :, shift : shift + BLOCK]
+                    far = far * scale + skewed[2 * head + 1, :, shift : shift + BLOCK]
+                    highest = jnp.max(jnp.maximum(near, far), axis=1, keepdims=True)
+                    near = jnp.exp2(near - highest).astype(jnp.bfloat16)
+                    far = jnp.exp2(far - highest).astype(jnp.bfloat16)
+                    summed = jnp.dot(
+                        near, near_values, preferred_element_type=jnp.float32
+                    ) + jnp.dot(far, far_values, preferred_element_type=jnp.float32)
+                    target[rows_here, columns] = (summed[:, :LANES] / summed[:, LANES:]).astype(
+                        jnp.bfloat16
+                    )
+            return carry
+
+        lax.fori_loop(0, half_heads // GROUP, body, 0)
+
+    whole_rows = pl.ds(pl.multiple_of(odd * HALF, HALF), BLOCK)
+    side_width = half_heads * LANES
+
+    def store_whole(side):
+        columns = pl.ds(side * side_width, side_width)
+        return pltpu.make_async_copy(
+            whole_out.at[:, columns], out_ref.at[whole_rows, columns], out_sem.at[side]
+        )
+
+    own_columns = pl.ds(pl.multiple_of(odd * side_width, LANES), side_width)
+    own_place = out_ref.at[pl.ds(pl.multiple_of(2 * HALF * (1 - odd), HALF), HALF), own_columns]
+    store_middle = pltpu.make_async_copy(
+        middle_out.at[pl.ds(pl.multiple_of(odd * HALF, HALF), HALF), :], own_place, out_sem.at[2]
+    )
+    swap_middle = pltpu.make_async_remote_copy(
+        src_ref=middle_out.at[pl.ds(pl.multiple_of((1 - odd) * HALF, HALF), HALF), :],
+        dst_ref=out_ref.at[pl.ds(pl.multiple_of(2 * HALF * odd, HALF), HALF), own_columns],
+        send_sem=swap_send,
+        recv_sem=swap_recv,
+        device_id=place_of(plane, pair),
+        device_id_type=MESH,
+    )
+    loads = [
+        pltpu.make_async_copy(source.at[whole_rows, :], target, whole_sem.at[i])
+        for i, (source, target) in enumerate(((q_ref, whole_q), (k_ref, whole_k), (v_ref, whole_v)))
+    ]
 
     for chunk in range(SLOTS):
         fan_out(chunk)
@@ -252,6 +337,8 @@
             device_id_type=MESH,
         ).start()
         pltpu.make_async_copy(source.at[half_rows, own], place, half_recv.at[i]).start()
+    for load in loads:
+        load.start()
     for chunk in range(SLOTS):
         finish(fanned.at[chunk], z1_recv.at[chunk])
         by_head(chunk)
@@ -261,7 +348,7 @@
         for slot in range(SLOTS):
             part = held.at[pl.ds(slot * PLANE_DEVICES * PLANES, PLANE_DEVICES * PLANES)]
             finish(part, p1_recv.at[kind * SLOTS + slot])
-        for slot in range(SLOTS):
+        for slot in (1, 0, 2):
             pick(kind, slot)
             send_picked(kind * SLOTS + slot)
         if kind == 0:
@@ -270,11 +357,27 @@
                 finish(fanned.at[chunk], z1_recv.at[chunk])
                 by_head(chunk)
             skew_rows()
-    for chunk in range(2 * SLOTS):
+    for slot in (1, 0, 2):
+        finish(landed.at[slot], z2_recv.at[slot])
+        deliver(slot)
+    for slot in (1, 0, 2):
+        chunk = SLOTS + slot
         finish(landed.at[chunk], z2_recv.at[chunk])
         deliver(chunk)
+        finish(far_ref.at[slot], p2_recv.at[slot])
+        finish(far_ref.at[chunk], p2_recv.at[chunk])
+        if slot == 1:
+            for i, target in enumerate((mid_q_ref, mid_k_ref, mid_v_ref)):
+                finish(target, half_recv.at[i])
+            for load in loads:
+                load.wait()
+        attend(slot)
+        if slot == 1:
+            store_middle.start()
+            swap_middle.start()
+        else:
+            store_whole(slot // 2).start()
     for i, target in enumerate((mid_q_ref, mid_k_ref, mid_v_ref)):
-        finish(target, half_recv.at[i])
         finish(target.at[pl.ds(0, HALF), :], half_send.at[i])
     for chunk in range(2 * SLOTS):
         finish(fanned.at[chunk, pl.ds(0, PLANES - 1)], z1_send.at[chunk])
@@ -283,9 +386,10 @@
         finish(far_ref.at[chunk, pl.ds(0, PLANE_DEVICES - 1)], p2_send.at[chunk])
     finish(rows.at[pl.ds(0, 3 * ROW_SET)], row_send.at[0])
     finish(near_rows, row_send.at[1])
-    finish(skew_ref, skew_sem)
-    for chunk in range(2 * SLOTS):
-        finish(far_ref.at[chunk], p2_recv.at[chunk])
+    store_middle.wait()
+    swap_middle.wait()
+    store_whole(0).wait()
+    store_whole(1).wait()
 
 
 def move_tiles(table, queries, keys, values, own_rows):
@@ -293,29 +397,28 @@
     kind = keys.dtype
     chunks = 2 * SLOTS
     tiles = SLOTS * PLANES * PLANE_DEVICES
-    middle = jax.ShapeDtypeStruct((BLOCK, columns // 2), kind)
     anywhere = pl.BlockSpec(memory_space=pltpu.HBM)
-    semaphores = [pltpu.SemaphoreType.DMA((2,))] * 2 + [pltpu.SemaphoreType.DMA]
-    semaphores += [pltpu.SemaphoreType.DMA((3,))] * 2 + [pltpu.SemaphoreType.DMA((chunks,))] * 8
+    semaphores = (
+        [pltpu.SemaphoreType.DMA((2,))] * 2
+        + [pltpu.SemaphoreType.DMA((3,))] * 2
+        + [pltpu.SemaphoreType.DMA] * 2
+        + [pltpu.SemaphoreType.DMA((3,))] * 2
+        + [pltpu.SemaphoreType.DMA((chunks,))] * 8
+    )
     return pl.pallas_call(
         move_kernel,
         in_specs=[pl.BlockSpec(memory_space=pltpu.SMEM)]
         + [anywhere] * 3
         + [pl.BlockSpec(memory_space=pltpu.VMEM)],
-        out_specs=[anywhere] * 5,
-        out_shape=[
-            jax.ShapeDtypeStruct((chunks, PLANE_DEVICES, PLANES, ROWS, LANES), kind),
-            middle,
-            middle,
-            middle,
-            jax.ShapeDtypeStruct((2 * HEADS, HALF, BLOCK + HALF), jnp.float32),
-        ],
-        scratch_shapes=[
-            pltpu.VMEM((chunks, PLANES, ROWS, columns), kind),
-            pltpu.VMEM((tiles, ROWS, LANES), kind),
-            pltpu.VMEM((tiles, ROWS, LANES), kind),
-            pltpu.VMEM((tiles, ROWS, LANES), kind),
-            pltpu.VMEM((tiles, ROWS, LANES), kind),
+        out_specs=anywhere,
+        out_shape=jax.ShapeDtypeStruct((rows, columns), kind),
+        scratch_shapes=[pltpu.VMEM((chunks, PLANE_DEVICES, PLANES, ROWS, LANES), kind)]
+        + [pltpu.VMEM((BLOCK, columns // 2), kind)] * 3
+        + [pltpu.VMEM((BLOCK, columns), kind)] * 4
+        + [pltpu.VMEM((BLOCK, columns // 2), kind)]
+        + [pltpu.VMEM((chunks, PLANES, ROWS, columns), kind)]
+        + [pltpu.VMEM((tiles, ROWS, LANES), kind)] * 4
+        + [
             pltpu.VMEM((chunks, PLANES, PLANE_DEVICES, ROWS, LANES), kind),
             pltpu.VMEM((2 * HEADS, 2 * BLOCK), jnp.float32),
             pltpu.VMEM((2 * HEADS, HALF, BLOCK + HALF), jnp.float32),
@@ -325,126 +428,10 @@
             flops=0, transcendentals=0, bytes_accessed=1024 * 1024 * 1024
         ),
         compiler_params=pltpu.CompilerParams(
-            collective_id=0, has_side_effects=True, vmem_limit_bytes=48 * 1024 * 1024
+            collective_id=0, has_side_effects=True, vmem_limit_bytes=60 * 1024 * 1024
         ),
         name="move_tiles",
     )(table, queries, keys, values, own_rows)
-
-
-def attend_kernel(parity_ref, q, k, v, ka, kb, va, vb, skew, out_ref):
-    scale = math.log2(math.e) / math.sqrt(LANES)
-    contract = (((1,), (1,)), ((), ()))
-    ones = jnp.ones((BLOCK, LANES), jnp.bfloat16)
-    for g in range(GROUP):
-        columns = slice(g * LANES, (g + 1) * LANES)
-        near_keys = k[:, columns]
-        far_keys = jnp.concatenate([half[0, g].reshape(HALF, LANES) for half in (ka, kb)], axis=0)
-        far_values = jnp.concatenate([half[0, g].reshape(HALF, LANES) for half in (va, vb)], axis=0)
-        near_values = jnp.concatenate([v[:, columns], ones], axis=1)
-        far_values = jnp.concatenate([far_values, ones], axis=1)
-        for half in range(2):
-            shift = HALF * (1 - half)
-            rows = slice(half * HALF, (half + 1) * HALF)
-            query = q[rows, columns]
-            near = lax.dot_general(query, near_keys, contract, preferred_element_type=jnp.float32)
-            far = lax.dot_general(query, far_keys, contract, preferred_element_type=jnp.float32)
-            near = near * scale + skew[2 * g, :, shift : shift + BLOCK]
-            far = far * scale + skew[2 * g + 1, :, shift : shift + BLOCK]
-            highest = jnp.max(jnp.maximum(near, far), axis=1, keepdims=True)
-            near = jnp.exp2(near - highest).astype(jnp.bfloat16)
-            far = jnp.exp2(far - highest).astype(jnp.bfloat16)
-            summed = jnp.dot(near, near_values, preferred_element_type=jnp.float32) + jnp.dot(
-                far, far_values, preferred_element_type=jnp.float32
-            )
-            out_ref[rows, columns] = (summed[:, :LANES] / summed[:, LANES:]).astype(jnp.bfloat16)
-
-
-def attend(parity, queries, keys, values, far, skewed, middle):
-    width = GROUP * LANES
-    half_steps = HEADS // 2 // GROUP
-    steps = half_steps if middle else 2 * half_steps
-
-    def group_of(i, e):
-        return i + half_steps * e[0] if middle else i
-
-    def other_of(i, e):
-        return lax.rem(group_of(i, e) + half_steps, 2 * half_steps)
-
-    def slot_of(i):
-        return 1 if middle else 2 * (i // half_steps)
-
-    if middle:
-        local = pl.BlockSpec((BLOCK, width), lambda i, e: (0, i))
-    else:
-        local = pl.BlockSpec(
-            (pl.Element(BLOCK), pl.Element(width)), lambda i, e: (e[0] * HALF, i * width)
-        )
-    tiles = (1, GROUP, CHUNKS, ROWS, LANES)
-    return pl.pallas_call(
-        attend_kernel,
-        grid_spec=pltpu.PrefetchScalarGridSpec(
-            num_scalar_prefetch=1,
-            grid=(steps,),
-            in_specs=[
-                local,
-                local,
-                local,
-                pl.BlockSpec(tiles, lambda i, e: (slot_of(i), group_of(i, e), 0, 0, 0)),
-                pl.BlockSpec(tiles, lambda i, e: (slot_of(i), other_of(i, e), 0, 0, 0)),
-                pl.BlockSpec(tiles, lambda i, e: (SLOTS + slot_of(i), group_of(i, e), 0, 0, 0)),
-                pl.BlockSpec(tiles, lambda i, e: (SLOTS + slot_of(i), other_of(i, e), 0, 0, 0)),
-                pl.BlockSpec(
-                    (2 * GROUP, HALF, BLOCK + HALF), lambda i, e: (group_of(i, e), 0, 0)
-                ),
-            ],
-            out_specs=local,
-        ),
-        out_shape=jax.ShapeDtypeStruct(queries.shape, jnp.bfloat16),
-        cost_estimate=pl.CostEstimate(
-            flops=steps * GROUP * 8 * BLOCK * BLOCK * LANES,
-            transcendentals=steps * GROUP * 2 * BLOCK * BLOCK,
-            bytes_accessed=steps * 4 * 1024 * 1024,
-        ),
-        compiler_params=pltpu.CompilerParams(vmem_limit_bytes=60 * 1024 * 1024),
-        name="attend_middle" if middle else "attend_whole",
-    )(parity, queries, keys, values, far, far, far, far, skewed)
-
-
-def place_kernel(parity_ref, own_ref, other_ref, into_ref, out_ref, sems):
-    odd = parity_ref[0]
-    width = own_ref.shape[1]
-    rows = pl.ds(pl.multiple_of(2 * HALF * (1 - odd), HALF), HALF)
-    own = pltpu.make_async_copy(
-        own_ref.at[pl.ds(pl.multiple_of(odd * HALF, HALF), HALF), :],
-        out_ref.at[rows, pl.ds(pl.multiple_of(odd * width, LANES), width)],
-        sems.at[0],
-    )
-    other = pltpu.make_async_copy(
-        other_ref,
-        out_ref.at[rows, pl.ds(pl.multiple_of((1 - odd) * width, LANES), width)],
-        sems.at[1],
-    )
-    own.start()
-    other.start()
-    own.wait()
-    other.wait()
-
-
-def place_half(parity, own, other, into):
-    anywhere = pl.BlockSpec(memory_space=pltpu.HBM)
-    return pl.pallas_call(
-        place_kernel,
-        in_specs=[pl.BlockSpec(memory_space=pltpu.SMEM)] + [anywhere] * 3,
-        out_specs=anywhere,
-        out_shape=jax.ShapeDtypeStruct(into.shape, into.dtype),
-        scratch_shapes=[pltpu.SemaphoreType.DMA((2,))],
-        input_output_aliases={3: 0},
-        cost_estimate=pl.CostEstimate(
-            flops=0, transcendentals=0, bytes_accessed=4 * HALF * own.shape[1] * 2
-        ),
-        compiler_params=pltpu.CompilerParams(vmem_limit_bytes=60 * 1024 * 1024),
-        name="place_half",
-    )(parity, own, other, into)
 
 
 def tile_table(partner):
@@ -464,24 +451,15 @@
 
 
 def on_device(queries, key_states, value_states, partner, buckets, bias_table):
-    odd = lax.rem(lax.axis_index("head"), 2).astype(jnp.int32)
-    parity = odd.reshape(1)
-
     one_hot = (
         buckets[..., None] == jnp.arange(bias_table.shape[0], dtype=jnp.int32)
     ).astype(jnp.float32)
     own_rows = jnp.einsum("skb,bh->hsk", one_hot, bias_table, precision=lax.Precision.HIGHEST)
     own_rows = jnp.pad(own_rows * math.log2(math.e), ((0, 0), (0, 0), (0, 1)))
 
-    far, mid_q, mid_k, mid_v, skewed = move_tiles(
+    return move_tiles(
         tile_table(partner), queries, key_states, value_states, own_rows.reshape(ROW_SET, 2 * BLOCK)
     )
-    middle = attend(parity, mid_q, mid_k, mid_v, far, skewed, True)
-    outgoing = lax.dynamic_slice_in_dim(middle, (1 - odd) * HALF, HALF, 0)
-    swap = [(i, i ^ 1) for i in range(lax.axis_size("head"))]
-    incoming = lax.ppermute(outgoing, "head", swap)
-    out = attend(parity, queries, key_states, value_states, far, skewed, False)
-    return place_half(parity, middle, incoming, out)
 
 
 def solution(mesh):

time: 369 us -> 331 us (0.90)
  Pallas kernels: 361 us -> 324 us
    pallas_call x3 -> x0, Pallas kernels: 54.3 us -> none  [the longest x1 32.9 us: place_half(): pl.pallas_call(place_kernel, in_specs=[pl.BlockSpec(memory_space=pltpu.SM...]
    pallas_call x1, Pallas kernels: 307 us -> 324 us  [move_tiles(): pl.pallas_call(move_kernel, in_specs=[pl.BlockSpec(memory_space=pltpu.SME...]
  transfers between devices with their start and end apart: 1 -> 0, of which waited for: 0 -> 0; matrix products, arithmetic and copies ran while one was open for 0% -> 0% of each run, Pallas kernels for 4% -> 0%
where the time goes in v4:
time: 331 us; the launch traced here: 330 us
  Pallas kernels  324 us (98%)
  local copies, waits for them, and re-layouts  4.55 us (1%)
    pallas_call x1, Pallas kernels, move_tiles(): pl.pallas_call(move_kernel, in_specs=[pl.BlockSpec(memory_space=pltpu.SME...  324 us

profile of v4, /device:TPU:1, one launch (start us, length us, event | category | flops | bytes accessed | tf_op | source)
XLA Modules:
  0.0 330.3 jit_solution(2132063687167889261)
XLA Ops:
  0.0 0.0 copy-start
  0.0 0.7 fusion.6
  0.7 0.6 pad_add_fusion.table_ref
  1.3 0.0 copy-done
  1.3 0.8 fusion
  2.2 0.6 reshape.4.row_ref
  2.8 323.5 %move_tiles.1 = bf16[384,4096]{1,0:T(8,128)(2,1)} custom-call(s32[768]{0:T(1024)} %pad_add_fusion.table_ref, bf16[384,4096]{1,0:T(8,128)(2,1)} %q_ref.1, bf16[384,4096]{1,0:T(8,128)(2,1)} %k_ref.1, bf16[384,4096]{1,0:T(8,128)(2,1)} %v_ref.1, f32[8,512]{1,0:T(8,128)} %reshape.4.row_ref), custom_call_target="tpu_custom_call" | custom-call | bytes 1073741824 | tf_op jit(solution)/shard_map/move_tiles/pallas_call | solution.py:408
  326.4 3.9 %copy.10 = bf16[384,4096]{1,0:T(8,128)(2,1)} copy(bf16[384,4096]{1,0:T(8,128)(2,1)} %move_tiles.1) | data formatting | bytes 6291456
  (2 shorter events, 0.0 us)
Async XLA Ops:
  0.0 1.3 copy-start

commit v5 on v4

--- a/solution.py
+++ b/solution.py
@@ -21,6 +21,7 @@
 PLANE_DEVICES = 32
 SLOTS = 3
 ROW_SET = 8
+ORDER = (1, 0, 2)
 
 
 def place_of(plane, spot):
@@ -43,6 +44,7 @@
     whole_v,
     whole_out,
     middle_out,
+    weights,
     fanned,
     held_k,
     held_v,
@@ -164,34 +166,35 @@
 
         def body(z, carry):
             first = (z // 2) * 96 + lax.rem(z, 2) * 6
-            base = (slot * PLANES + z) * PLANE_DEVICES
+            base = slot * PLANES * PLANE_DEVICES + z
             for p in range(PLANE_DEVICES):
                 e = p % 2
                 low = (True, e == 0, False)[slot]
                 member = 1 if slot == 1 else 2 * e
                 block = first + (p // 4) * 12 + (p % 4 // 2) * 3 + member
                 chosen = side if low else 1 - side
-                picked[base + p] = held[table_ref[chosen * blocks + block]]
+                picked[base + p * PLANES] = held[table_ref[chosen * blocks + block]]
             return carry
 
         lax.fori_loop(0, PLANES, body, 0)
 
-    def send_picked(chunk):
+    def share_picked(chunk):
         kind, slot = divmod(chunk, SLOTS)
         picked = (picked_k, picked_v)[kind]
+        plane_stage(
+            lambda other: picked.at[pl.ds((slot * PLANE_DEVICES + other) * PLANES, PLANES)],
+            landed.at[chunk, :, spot],
+            p2_send.at[chunk],
+            p2_recv.at[chunk],
+        )
+
+    def deliver(chunk):
+        finish(landed.at[chunk], p2_recv.at[chunk])
         z_stage(
-            lambda other: picked.at[pl.ds((slot * PLANES + other) * PLANE_DEVICES, PLANE_DEVICES)],
-            landed.at[chunk, plane],
+            lambda other: landed.at[chunk, other],
+            far_ref.at[chunk, plane],
             z2_send.at[chunk],
             z2_recv.at[chunk],
-        )
-
-    def deliver(chunk):
-        plane_stage(
-            lambda other: landed.at[chunk, :, other],
-            far_ref.at[chunk, spot],
-            p2_send.at[chunk],
-            p2_recv.at[chunk],
         )
 
     lower = lax.rem(plane, 2)
@@ -246,52 +249,80 @@
     contract = (((1,), (1,)), ((), ()))
     half_heads = HEADS // 2
 
+    ones = jnp.ones((BLOCK, LANES), jnp.bfloat16)
+
+    def far_block(chunk, head):
+        other = lax.rem(head + half_heads, HEADS)
+        return jnp.concatenate(
+            [far_ref[chunk, :, one].reshape(HALF, LANES) for one in (head, other)], axis=0
+        )
+
+    def weigh(query, near_keys, far_keys, head, half):
+        shift = HALF * (1 - half)
+        near = lax.dot_general(query, near_keys, contract, preferred_element_type=jnp.float32)
+        far = lax.dot_general(query, far_keys, contract, preferred_element_type=jnp.float32)
+        near = near * scale + skewed[2 * head, :, shift : shift + BLOCK]
+        far = far * scale + skewed[2 * head + 1, :, shift : shift + BLOCK]
+        highest = jnp.max(jnp.maximum(near, far), axis=1, keepdims=True)
+        return tuple(jnp.exp2(part - highest).astype(jnp.bfloat16) for part in (near, far))
+
+    def blend(near, far, near_values, far_values):
+        summed = jnp.dot(near, near_values, preferred_element_type=jnp.float32) + jnp.dot(
+            far, far_values, preferred_element_type=jnp.float32
+        )
+        return (summed[:, :LANES] / summed[:, LANES:]).astype(jnp.bfloat16)
+
+    def over_heads(slot, visit):
+        middle = slot == 1
+        first = (0, half_heads * odd, half_heads)[slot]
+
+        def body(i, carry):
+            for g in range(GROUP):
+                place = i * GROUP + g
+                start = (place if middle else first + place) * LANES
+                visit(place, first + place, pl.ds(pl.multiple_of(start, LANES), LANES))
+            return carry
+
+        lax.fori_loop(0, half_heads // GROUP, body, 0)
+
     def attend(slot):
         middle = slot == 1
-        first = (0, half_heads * odd, half_heads)[slot]
         q, k, v = (mid_q_ref, mid_k_ref, mid_v_ref) if middle else (whole_q, whole_k, whole_v)
         target = middle_out if middle else whole_out
-        ones = jnp.ones((BLOCK, LANES), jnp.bfloat16)
-
-        def body(i, carry):
-            for g in range(GROUP):
-                head = first + i * GROUP + g
-                other = lax.rem(head + half_heads, HEADS)
-                start = (i * GROUP + g if middle else head) * LANES
-                columns = pl.ds(pl.multiple_of(start, LANES), LANES)
-                near_keys = k[:, columns]
-                near_values = jnp.concatenate([v[:, columns], ones], axis=1)
-                far_keys, far_values = (
-                    jnp.concatenate(
-                        [far_ref[chunk, one].reshape(HALF, LANES) for one in (head, other)], axis=0
-                    )
-                    for chunk in (slot, SLOTS + slot)
-                )
-                far_values = jnp.concatenate([far_values, ones], axis=1)
-                for half in range(2):
-                    shift = HALF * (1 - half)
-                    rows_here = slice(half * HALF, (half + 1) * HALF)
-                    query = q[rows_here, columns]
-                    near = lax.dot_general(
-                        query, near_keys, contract, preferred_element_type=jnp.float32
-                    )
-                    far = lax.dot_general(
-                        query, far_keys, contract, preferred_element_type=jnp.float32
-                    )
-                    near = near * scale + skewed[2 * head, :, shift : shift + BLOCK]
-                    far = far * scale + skewed[2 * head + 1, :, shift : shift + BLOCK]
-                    highest = jnp.max(jnp.maximum(near, far), axis=1, keepdims=True)
-                    near = jnp.exp2(near - highest).astype(jnp.bfloat16)
-                    far = jnp.exp2(far - highest).astype(jnp.bfloat16)
-                    summed = jnp.dot(
-                        near, near_values, preferred_element_type=jnp.float32
-                    ) + jnp.dot(far, far_values, preferred_element_type=jnp.float32)
-                    target[rows_here, columns] = (summed[:, :LANES] / summed[:, LANES:]).astype(
-                        jnp.bfloat16
-                    )
-            return carry
-
-        lax.fori_loop(0, half_heads // GROUP, body, 0)
+
+        def visit(place, head, columns):
+            near_keys = k[:, columns]
+            far_keys = far_block(slot, head)
+            near_values = jnp.concatenate([v[:, columns], ones], axis=1)
+            far_values = jnp.concatenate([far_block(SLOTS + slot, head), ones], axis=1)
+            for half in range(2):
+                part = slice(half * HALF, (half + 1) * HALF)
+                near, far = weigh(q[part, columns], near_keys, far_keys, head, half)
+                target[part, columns] = blend(near, far, near_values, far_values)
+
+        over_heads(slot, visit)
+
+    def weigh_last():
+        def visit(place, head, columns):
+            near_keys = whole_k[:, columns]
+            far_keys = far_block(2, head)
+            for half in range(2):
+                part = slice(half * HALF, (half + 1) * HALF)
+                near, far = weigh(whole_q[part, columns], near_keys, far_keys, head, half)
+                weights[place, part, :BLOCK] = near
+                weights[place, part, BLOCK:] = far
+
+        over_heads(2, visit)
+
+    def blend_last():
+        def visit(place, head, columns):
+            near_values = jnp.concatenate([whole_v[:, columns], ones], axis=1)
+            far_values = jnp.concatenate([far_block(SLOTS + 2, head), ones], axis=1)
+            whole_out[:, columns] = blend(
+                weights[place, :, :BLOCK], weights[place, :, BLOCK:], near_values, far_values
+            )
+
+        over_heads(2, visit)
 
     whole_rows = pl.ds(pl.multiple_of(odd * HALF, HALF), BLOCK)
     side_width = half_heads * LANES
@@ -339,39 +370,42 @@
         pltpu.make_async_copy(source.at[half_rows, own], place, half_recv.at[i]).start()
     for load in loads:
         load.start()
+    def choose(kind):
+        held = (held_k, held_v)[kind]
+        for slot in range(SLOTS):
+            part = held.at[pl.ds(slot * PLANE_DEVICES * PLANES, PLANE_DEVICES * PLANES)]
+            finish(part, p1_recv.at[kind * SLOTS + slot])
+        for slot in ORDER:
+            pick(kind, slot)
+            share_picked(kind * SLOTS + slot)
+
     for chunk in range(SLOTS):
         finish(fanned.at[chunk], z1_recv.at[chunk])
         by_head(chunk)
         fan_out(chunk + SLOTS)
-    for kind in range(2):
-        held = (held_k, held_v)[kind]
-        for slot in range(SLOTS):
-            part = held.at[pl.ds(slot * PLANE_DEVICES * PLANES, PLANE_DEVICES * PLANES)]
-            finish(part, p1_recv.at[kind * SLOTS + slot])
-        for slot in (1, 0, 2):
-            pick(kind, slot)
-            send_picked(kind * SLOTS + slot)
-        if kind == 0:
-            share_rows()
-            for chunk in range(SLOTS, 2 * SLOTS):
-                finish(fanned.at[chunk], z1_recv.at[chunk])
-                by_head(chunk)
-            skew_rows()
-    for slot in (1, 0, 2):
-        finish(landed.at[slot], z2_recv.at[slot])
+    choose(0)
+    share_rows()
+    for i, slot in enumerate(ORDER):
+        finish(fanned.at[SLOTS + i], z1_recv.at[SLOTS + i])
+        by_head(SLOTS + i)
         deliver(slot)
-    for slot in (1, 0, 2):
-        chunk = SLOTS + slot
-        finish(landed.at[chunk], z2_recv.at[chunk])
-        deliver(chunk)
-        finish(far_ref.at[slot], p2_recv.at[slot])
-        finish(far_ref.at[chunk], p2_recv.at[chunk])
-        if slot == 1:
-            for i, target in enumerate((mid_q_ref, mid_k_ref, mid_v_ref)):
-                finish(target, half_recv.at[i])
-            for load in loads:
-                load.wait()
-        attend(slot)
+    skew_rows()
+    choose(1)
+    for slot in ORDER:
+        deliver(SLOTS + slot)
+    for slot in ORDER:
+        finish(far_ref.at[slot], z2_recv.at[slot])
+    for i, target in enumerate((mid_q_ref, mid_k_ref, mid_v_ref)):
+        finish(target, half_recv.at[i])
+    for load in loads:
+        load.wait()
+    weigh_last()
+    for slot in ORDER:
+        finish(far_ref.at[SLOTS + slot], z2_recv.at[SLOTS + slot])
+        if slot == 2:
+            blend_last()
+        else:
+            attend(slot)
         if slot == 1:
             store_middle.start()
             swap_middle.start()
@@ -381,9 +415,9 @@
         finish(target.at[pl.ds(0, HALF), :], half_send.at[i])
     for chunk in range(2 * SLOTS):
         finish(fanned.at[chunk, pl.ds(0, PLANES - 1)], z1_send.at[chunk])
-        finish(far_ref.at[chunk, pl.ds(0, PLANE_DEVICES - 1)], p1_send.at[chunk])
+        finish(landed.at[chunk, :, pl.ds(0, PLANE_DEVICES - 1)], p1_send.at[chunk])
+        finish(landed.at[chunk, :, pl.ds(0, PLANE_DEVICES - 1)], p2_send.at[chunk])
         finish(landed.at[chunk, pl.ds(0, PLANES - 1)], z2_send.at[chunk])
-        finish(far_ref.at[chunk, pl.ds(0, PLANE_DEVICES - 1)], p2_send.at[chunk])
     finish(rows.at[pl.ds(0, 3 * ROW_SET)], row_send.at[0])
     finish(near_rows, row_send.at[1])
     store_middle.wait()
@@ -412,10 +446,11 @@
         + [pl.BlockSpec(memory_space=pltpu.VMEM)],
         out_specs=anywhere,
         out_shape=jax.ShapeDtypeStruct((rows, columns), kind),
-        scratch_shapes=[pltpu.VMEM((chunks, PLANE_DEVICES, PLANES, ROWS, LANES), kind)]
+        scratch_shapes=[pltpu.VMEM((chunks, PLANES, PLANE_DEVICES, ROWS, LANES), kind)]
         + [pltpu.VMEM((BLOCK, columns // 2), kind)] * 3
         + [pltpu.VMEM((BLOCK, columns), kind)] * 4
         + [pltpu.VMEM((BLOCK, columns // 2), kind)]
+        + [pltpu.VMEM((HEADS // 2, BLOCK, 2 * BLOCK), kind)]
         + [pltpu.VMEM((chunks, PLANES, ROWS, columns), kind)]
         + [pltpu.VMEM((tiles, ROWS, LANES), kind)] * 4
         + [

time: 331 us -> 295 us (0.89)
  Pallas kernels: 324 us -> 288 us
    pallas_call x1, Pallas kernels: 324 us -> 288 us  [move_tiles(): pl.pallas_call(move_kernel, in_specs=[pl.BlockSpec(memory_space=pltpu.SME...]
where the time goes in v5:
time: 295 us; the launch traced here: 294 us
  Pallas kernels  288 us (98%)
  local copies, waits for them, and re-layouts  4.55 us (2%)
    pallas_call x1, Pallas kernels, move_tiles(): pl.pallas_call(move_kernel, in_specs=[pl.BlockSpec(memory_space=pltpu.SME...  288 us

profile of v5, /device:TPU:1, one launch (start us, length us, event | category | flops | bytes accessed | tf_op | source)
XLA Modules:
  0.0 294.5 jit_solution(2758862821116045544)
XLA Ops:
  0.0 0.0 copy-start
  0.0 0.7 fusion.6
  0.7 0.6 pad_add_fusion.table_ref
  1.3 0.0 copy-done
  1.3 0.8 fusion
  2.2 0.6 reshape.4.row_ref
  2.8 287.7 %move_tiles.1 = bf16[384,4096]{1,0:T(8,128)(2,1)} custom-call(s32[768]{0:T(1024)} %pad_add_fusion.table_ref, bf16[384,4096]{1,0:T(8,128)(2,1)} %q_ref.1, bf16[384,4096]{1,0:T(8,128)(2,1)} %k_ref.1, bf16[384,4096]{1,0:T(8,128)(2,1)} %v_ref.1, f32[8,512]{1,0:T(8,128)} %reshape.4.row_ref), custom_call_target="tpu_custom_call" | custom-call | bytes 1073741824 | tf_op jit(solution)/shard_map/move_tiles/pallas_call | solution.py:442
  290.6 3.9 %copy.10 = bf16[384,4096]{1,0:T(8,128)(2,1)} copy(bf16[384,4096]{1,0:T(8,128)(2,1)} %move_tiles.1) | data formatting | bytes 6291456
  (2 shorter events, 0.0 us)
Async XLA Ops:
  0.0 1.3 copy-start

commit v6 on v5

--- a/solution.py
+++ b/solution.py
@@ -469,6 +469,538 @@
     )(table, queries, keys, values, own_rows)
 
 
+PARTS = 4
+PIECE = BLOCK // PARTS
+HELD = 48
+ROOM = ((13, 10), (14, 11))
+HOPS = (2, 1, -1, -2)
+
+
+def room_starts(room):
+    far, near = room
+    return (0, far, far + near, far + 2 * near)
+
+
+def room_size(room):
+    return 2 * sum(room)
+
+
+def route_kernel(row_ref, column_ref, send_ref, relay_ref, final_ref, over_ref):
+    count = row_ref.shape[1]
+    i_row = lax.broadcasted_iota(jnp.int32, (1, count), 1)
+    i_column = lax.broadcasted_iota(jnp.int32, (count, 1), 0)
+
+    def both(f, *pairs):
+        return tuple(f(*(pair[s] for pair in pairs)) for s in range(2))
+
+    def rank(key):
+        same = key[1] == key[0]
+        in_row = jnp.sum(jnp.where(same & (i_column < i_row), 1.0, 0.0), axis=0, keepdims=True)
+        in_column = jnp.sum(jnp.where(same & (i_row < i_column), 1.0, 0.0), axis=1, keepdims=True)
+        return in_row.astype(jnp.int32), in_column.astype(jnp.int32)
+
+    block = (row_ref[...], column_ref[...])
+    seq = both(lambda m: m // 12, block)
+    rest = both(lambda m, s: m - 12 * s, block, seq)
+    source = both(lambda s, r: (s // 8) * 2 + jnp.where(r >= 6, 1, 0), seq, rest)
+    local = both(
+        lambda s, r: (s - 8 * (s // 8)) * 6 + jnp.where(r >= 6, r - 6, r), seq, rest
+    )
+    target = both(lambda i: i // HELD, (i_row, i_column))
+    ahead = both(lambda a, b: jnp.where(b >= a, b - a, b - a + PLANES), source, target)
+    turn = both(lambda r: r - 2 * (r // 2), rank(both(lambda a, b: a * 8 + b, source, target)))
+    sign = both(
+        lambda k, t: jnp.where(k < 4, 1, jnp.where((k == 4) & (t == 0), 1, -1)), ahead, turn
+    )
+    distance = both(lambda k: jnp.where(k <= 4, k, PLANES - k), ahead)
+    first = both(
+        lambda d, t: jnp.where(
+            d == 0,
+            0,
+            jnp.where(d == 1, t, jnp.where(d == 2, 2 * t, jnp.where(d == 3, 1 + t, 2))),
+        ),
+        distance,
+        turn,
+    )
+    second = both(lambda d, o: d - o, distance, first)
+    relay = both(
+        lambda z, s, o: jnp.bitwise_and(z + s * o + PLANES, PLANES - 1), source, sign, first
+    )
+
+    def slots(plane, hop, room):
+        way = both(lambda s, h: jnp.where(h == 0, 0, s * h), sign, hop)
+        order = rank(both(lambda p, w: p * 8 + w + 2, plane, way))
+        at = room_starts(room)
+        slot = both(
+            lambda w, r: r
+            + jnp.where(w == 2, at[0], jnp.where(w == 1, at[1], jnp.where(w == -1, at[2], at[3]))),
+            way,
+            order,
+        )
+        limit = jnp.where(hop[0] == 2, room[0], room[1])
+        over = jnp.where((way[0] != 0) & (order[0] >= limit), 1.0, 0.0)
+        return slot, jnp.sum(over, axis=1, keepdims=True)
+
+    slot_one, over_one = slots(source, first, ROOM[0])
+    slot_two, over_two = slots(relay, second, ROOM[1])
+    at_relay = both(lambda o, l, s: jnp.where(o == 0, l, HELD + s), first, local, slot_one)
+
+    def fill(out_ref, plane, hop, slot, room, value):
+        size = room_size(room)
+        place = lax.broadcasted_iota(jnp.int32, (1, PLANES * size), 1)
+        code = jnp.where(hop[1] == 0, -1, plane[1] * size + slot[1])
+        chosen = jnp.where(code == place, value[1].astype(jnp.float32), 0.0)
+        out_ref[...] = jnp.sum(chosen, axis=0, keepdims=True).astype(jnp.int32)
+
+    fill(send_ref, source, first, slot_one, ROOM[0], local)
+    fill(relay_ref, relay, second, slot_two, ROOM[1], at_relay)
+    final_ref[...] = jnp.where(
+        second[0] == 0, at_relay[0], HELD + room_size(ROOM[0]) + slot_two[0]
+    )
+    over_ref[...] = (over_one + over_two).astype(jnp.int32)
+
+
+def plan_routes(partner):
+    order = partner.reshape(4, 8, 2, 6).transpose(0, 2, 1, 3).reshape(-1)
+    full = pl.BlockSpec(memory_space=pltpu.VMEM)
+    shapes = [(1, PLANES * room_size(room)) for room in ROOM] + [(1, order.shape[0]), (1, 1)]
+    return pl.pallas_call(
+        route_kernel,
+        in_specs=[full] * 2,
+        out_specs=[full] * 4,
+        out_shape=[jax.ShapeDtypeStruct(shape, jnp.int32) for shape in shapes],
+        name="plan_routes",
+    )(order.reshape(1, -1), order.reshape(-1, 1))
+
+
+def short_kernel(
+    send_ref, relay_ref, final_ref, q_ref, k_ref, v_ref, row_ref, out_ref, *scratch
+):
+    chunks = 2 * PARTS
+    held, near_in, far_in = (scratch[i * chunks : (i + 1) * chunks] for i in range(3))
+    (
+        staged_one,
+        staged_two,
+        staged_out,
+        far_ref,
+        weights_f,
+        weights_b,
+        all_q,
+        full_k,
+        full_v,
+        mid_k,
+        mid_v,
+        all_out,
+        rows,
+        row_send,
+        row_recv,
+        load_sem,
+        out_sem,
+        half_send,
+        half_recv,
+        p0_send,
+        p0b_send,
+        p0_recv,
+        z1_send,
+        z1_recv,
+        z2_send,
+        z2_recv,
+        out_send,
+        out_recv,
+    ) = scratch[3 * chunks :]
+    seq = lax.axis_index("seq")
+    head = lax.axis_index("head")
+    plane = 2 * (seq // 8) + head // 4
+    spot = lax.rem(seq, 8) * 4 + lax.rem(head, 4)
+    odd = lax.rem(head, 2)
+    pair = spot + 1 - 2 * odd
+
+    def above(hop):
+        return lax.rem(plane + hop + PLANES, PLANES)
+
+    barrier = pltpu.get_barrier_semaphore()
+    for hop in HOPS:
+        pl.semaphore_signal(
+            barrier, inc=1, device_id=place_of(above(hop), spot), device_id_type=MESH
+        )
+
+    def greet(step, carry):
+        pl.semaphore_signal(
+            barrier,
+            inc=1,
+            device_id=place_of(plane, lax.rem(spot + step, PLANE_DEVICES)),
+            device_id_type=MESH,
+        )
+        return carry
+
+    lax.fori_loop(1, PLANE_DEVICES, greet, 0)
+    pl.semaphore_wait(barrier, len(HOPS) + PLANE_DEVICES - 1)
+
+    def finish(ref, sem):
+        pltpu.make_async_copy(ref, ref, sem).wait()
+
+    def plane_stage(source, target, send, recv):
+        def body(step, carry):
+            other = lax.rem(spot + step, PLANE_DEVICES)
+            pltpu.make_async_remote_copy(
+                src_ref=source(other),
+                dst_ref=target,
+                send_sem=send,
+                recv_sem=recv,
+                device_id=place_of(plane, other),
+                device_id_type=MESH,
+            ).start()
+            return carry
+
+        lax.fori_loop(1, PLANE_DEVICES, body, 0)
+        pltpu.make_async_copy(source(spot), target, recv).start()
+
+    def first_block(place):
+        return (place // 4) * 6 + (lax.rem(place, 4) // 2) * 3
+
+    full_rows = pl.ds(pl.multiple_of(odd * HALF, HALF), BLOCK)
+    half_rows = pl.ds(pl.multiple_of(2 * HALF * (1 - odd), HALF), HALF)
+
+    def spread(chunk):
+        kind, part = divmod(chunk, PARTS)
+        ref = (k_ref, v_ref)[kind]
+
+        def piece(start):
+            lines = pl.ds(pl.multiple_of(start, PIECE), PIECE)
+            return lambda other: ref.at[
+                lines, pl.ds(pl.multiple_of(other * LANES, LANES), LANES)
+            ]
+
+        plane_stage(
+            piece(odd * HALF + PIECE * part),
+            held[chunk].at[first_block(spot) + 2 * odd],
+            p0_send.at[chunk],
+            p0_recv.at[chunk],
+        )
+
+        @pl.when(odd == part // 2)
+        def _():
+            plane_stage(
+                piece(2 * HALF * (1 - odd) + PIECE * (part % 2)),
+                held[chunk].at[first_block(spot) + 1],
+                p0b_send.at[chunk],
+                p0_recv.at[chunk],
+            )
+
+    def z_stage(staged, landed, room, send, recv):
+        for start, size, hop in zip(room_starts(room), (*room, *room[::-1]), HOPS):
+            pltpu.make_async_remote_copy(
+                src_ref=staged.at[pl.ds(start, size)],
+                dst_ref=landed.at[pl.ds(start, size)],
+                send_sem=send,
+                recv_sem=recv,
+                device_id=place_of(above(hop), spot),
+                device_id_type=MESH,
+            ).start()
+
+    size_one, size_two = (room_size(room) for room in ROOM)
+
+    def leg_one(chunk):
+        finish(held[chunk], p0_recv.at[chunk])
+        slot = chunk % 2
+        if chunk >= 2:
+            finish(staged_one.at[slot], z1_send.at[chunk - 2])
+
+        def body(i, carry):
+            for j in range(2):
+                where = 2 * i + j
+                staged_one[slot, where] = held[chunk][send_ref[0, plane * size_one + where]]
+            return carry
+
+        lax.fori_loop(0, size_one // 2, body, 0)
+        z_stage(staged_one.at[slot], near_in[chunk], ROOM[0], z1_send.at[chunk], z1_recv.at[chunk])
+
+    def held_or_near(chunk, index):
+        kept = held[chunk][jnp.minimum(index, HELD - 1)]
+        came = near_in[chunk][jnp.clip(index - HELD, 0, size_one - 1)]
+        return jnp.where(index < HELD, kept, came)
+
+    def leg_two(chunk):
+        finish(near_in[chunk], z1_recv.at[chunk])
+        slot = chunk % 2
+        if chunk >= 2:
+            finish(staged_two.at[slot], z2_send.at[chunk - 2])
+
+        def body(i, carry):
+            for j in range(2):
+                where = 2 * i + j
+                index = relay_ref[0, plane * size_two + where]
+                staged_two[slot, where] = held_or_near(chunk, index)
+            return carry
+
+        lax.fori_loop(0, size_two // 2, body, 0)
+        z_stage(staged_two.at[slot], far_in[chunk], ROOM[1], z2_send.at[chunk], z2_recv.at[chunk])
+
+    def arrived(chunk, count=PLANE_DEVICES):
+        kind, part = divmod(chunk, PARTS)
+        return far_ref.at[kind, pl.ds(0, count), :, pl.ds(part * PIECE, PIECE)]
+
+    done = set()
+
+    def finish_far(chunk):
+        if chunk not in done:
+            done.add(chunk)
+            finish(arrived(chunk), out_recv.at[chunk])
+
+    def deliver(chunk):
+        finish(far_in[chunk], z2_recv.at[chunk])
+        slot = chunk % 2
+        if chunk >= 2:
+            finish(arrived(chunk - 2, PLANE_DEVICES - 1), out_send.at[chunk - 2])
+            finish_far(chunk - 2)
+        border = HELD + size_one
+
+        def body(i, carry):
+            for j in range(2):
+                where = 2 * i + j
+                index = final_ref[0, plane * HELD + where]
+                last = far_in[chunk][jnp.clip(index - border, 0, size_two - 1)]
+                staged_out[slot, where] = jnp.where(
+                    index < border, held_or_near(chunk, index), last
+                )
+            return carry
+
+        lax.fori_loop(0, HELD // 2, body, 0)
+        kind, part = divmod(chunk, PARTS)
+        plane_stage(
+            lambda other: staged_out.at[slot, pl.ds(first_block(other) + lax.rem(other, 2), 2)],
+            far_ref.at[kind, spot, :, pl.ds(part * PIECE, PIECE)],
+            out_send.at[chunk],
+            out_recv.at[chunk],
+        )
+
+    lower = lax.rem(plane, 2)
+    set_rows = 4 * ROW_SET
+    near_rows = rows.at[pl.ds(pl.multiple_of(lower * set_rows, ROW_SET), set_rows)]
+    far_rows = rows.at[pl.ds(pl.multiple_of((1 - lower) * set_rows, ROW_SET), set_rows)]
+    own_rows = rows.at[pl.ds(pl.multiple_of(head * ROW_SET, ROW_SET), ROW_SET)]
+
+    def show_rows():
+        for step in range(1, 4):
+            other = spot - lax.rem(spot, 4) + lax.rem(spot + step, 4)
+            pltpu.make_async_remote_copy(
+                src_ref=row_ref,
+                dst_ref=own_rows,
+                send_sem=row_send.at[0],
+                recv_sem=row_recv.at[0],
+                device_id=place_of(plane, other),
+                device_id_type=MESH,
+            ).start()
+        pltpu.make_async_copy(row_ref, own_rows, row_recv.at[0]).start()
+
+    def share_rows():
+        finish(near_rows, row_recv.at[0])
+        pltpu.make_async_remote_copy(
+            src_ref=near_rows,
+            dst_ref=near_rows,
+            send_sem=row_send.at[1],
+            recv_sem=row_recv.at[1],
+            device_id=place_of(plane + 1 - 2 * lower, spot),
+            device_id_type=MESH,
+        ).start()
+
+    loads = [
+        pltpu.make_async_copy(source, target, load_sem.at[i])
+        for i, (source, target) in enumerate(
+            ((q_ref, all_q), (k_ref.at[full_rows, :], full_k), (v_ref.at[full_rows, :], full_v))
+        )
+    ]
+
+    def swap_halves():
+        for i, (source, target) in enumerate(((k_ref, mid_k), (v_ref, mid_v))):
+            place = target.at[pl.ds(pl.multiple_of(odd * HALF, HALF), HALF), :]
+            pltpu.make_async_remote_copy(
+                src_ref=source.at[half_rows, :],
+                dst_ref=place,
+                send_sem=half_send.at[i],
+                recv_sem=half_recv.at[i],
+                device_id=place_of(plane, pair),
+                device_id_type=MESH,
+            ).start()
+            pltpu.make_async_copy(source.at[half_rows, :], place, half_recv.at[i]).start()
+
+    scale = math.log2(math.e) / math.sqrt(LANES)
+    contract = (((1,), (1,)), ((), ()))
+    ones = jnp.ones((BLOCK, LANES), jnp.bfloat16)
+
+    def weigh(query, near_keys, far_keys, near_bias, far_bias):
+        near = lax.dot_general(query, near_keys, contract, preferred_element_type=jnp.float32)
+        far = lax.dot_general(query, far_keys, contract, preferred_element_type=jnp.float32)
+        near = near * scale + near_bias
+        far = far * scale + far_bias
+        highest = jnp.max(jnp.maximum(near, far), axis=1, keepdims=True)
+        return tuple(jnp.exp2(part - highest).astype(jnp.bfloat16) for part in (near, far))
+
+    def skew(line):
+        return pltpu.roll(
+            jnp.broadcast_to(line, (HALF, 2 * BLOCK)),
+            2 * BLOCK - HALF + 1,
+            1,
+            stride=1,
+            stride_axis=0,
+        )
+
+    def weigh_heads(first, last):
+        def body(i, carry):
+            lines = rows[pl.ds(pl.multiple_of(i * ROW_SET, ROW_SET), ROW_SET), :]
+            for g in range(GROUP):
+                one = i * GROUP + g
+                columns = pl.ds(pl.multiple_of(one * LANES, LANES), LANES)
+                skews = [skew(lines[2 * g + side : 2 * g + side + 1]) for side in range(2)]
+                upper = [turned[:, HALF : HALF + BLOCK] for turned in skews]
+                under = [turned[:, :BLOCK] for turned in skews]
+                near_keys = full_k[:, columns]
+                far_keys = far_ref[0, one, odd]
+                for half in range(2):
+                    lines_here = pl.ds(pl.multiple_of((odd + half) * HALF, HALF), HALF)
+                    near, far = weigh(
+                        all_q[lines_here, columns], near_keys, far_keys, *(upper, under)[half]
+                    )
+                    part = slice(half * HALF, (half + 1) * HALF)
+                    weights_f[one, part, :BLOCK] = near
+                    weights_f[one, part, BLOCK:] = far
+                mixed = [jnp.where(odd == 1, u, o) for u, o in zip(under, upper)]
+                near, far = weigh(
+                    all_q[half_rows, columns], mid_k[:, columns], far_ref[0, one, 1 - odd], *mixed
+                )
+                weights_b[one, :, :BLOCK] = near
+                weights_b[one, :, BLOCK:] = far
+            return carry
+
+        lax.fori_loop(first // GROUP, last // GROUP, body, 0)
+
+    def blend(weights, near_values, far_values):
+        summed = jnp.dot(
+            weights[:, :BLOCK],
+            jnp.concatenate([near_values, ones], axis=1),
+            preferred_element_type=jnp.float32,
+        ) + jnp.dot(
+            weights[:, BLOCK:],
+            jnp.concatenate([far_values, ones], axis=1),
+            preferred_element_type=jnp.float32,
+        )
+        return (summed[:, :LANES] / summed[:, LANES:]).astype(jnp.bfloat16)
+
+    def blend_heads(first, last):
+        def body(i, carry):
+            for g in range(GROUP):
+                one = i * GROUP + g
+                columns = pl.ds(pl.multiple_of(one * LANES, LANES), LANES)
+                all_out[full_rows, columns] = blend(
+                    weights_f[one], full_v[:, columns], far_ref[1, one, odd]
+                )
+                all_out[half_rows, columns] = blend(
+                    weights_b[one], mid_v[:, columns], far_ref[1, one, 1 - odd]
+                )
+            return carry
+
+        lax.fori_loop(first // GROUP, last // GROUP, body, 0)
+
+    spread(0)
+    spread(1)
+    show_rows()
+    for load in loads:
+        load.start()
+    for step in range(chunks + 2):
+        if step < chunks:
+            leg_one(step)
+            if step + 2 < chunks:
+                spread(step + 2)
+        if step == 1:
+            share_rows()
+            swap_halves()
+        if 1 <= step <= chunks:
+            leg_two(step - 1)
+        if step >= 2:
+            deliver(step - 2)
+        turn = step - chunks + 2
+        if turn == 0:
+            for chunk in range(PARTS):
+                finish_far(chunk)
+            finish(mid_k, half_recv.at[0])
+            finish(mid_v, half_recv.at[1])
+            finish(far_rows, row_recv.at[1])
+            for load in loads:
+                load.wait()
+        if turn >= 0:
+            weigh_heads(turn * HEADS // 4, (turn + 1) * HEADS // 4)
+    finish_far(chunks - 2)
+    finish_far(chunks - 1)
+    stores = []
+    for side in range(2):
+        blend_heads(side * HEADS // 2, (side + 1) * HEADS // 2)
+        columns = pl.ds(side * HEADS // 2 * LANES, HEADS // 2 * LANES)
+        store = pltpu.make_async_copy(
+            all_out.at[:, columns], out_ref.at[:, columns], out_sem.at[side]
+        )
+        store.start()
+        stores.append(store)
+    for chunk in range(chunks):
+        finish(arrived(chunk, PLANE_DEVICES - 1).at[:, 0], p0_send.at[chunk])
+
+        @pl.when(odd == chunk % PARTS // 2)
+        def _():
+            finish(arrived(chunk, PLANE_DEVICES - 1).at[:, 0], p0b_send.at[chunk])
+
+    for chunk in range(chunks - 2, chunks):
+        finish(staged_one.at[chunk % 2], z1_send.at[chunk])
+        finish(staged_two.at[chunk % 2], z2_send.at[chunk])
+        finish(arrived(chunk, PLANE_DEVICES - 1), out_send.at[chunk])
+    for i, target in enumerate((mid_k, mid_v)):
+        finish(target.at[pl.ds(0, HALF), :], half_send.at[i])
+    finish(rows.at[pl.ds(0, 3 * ROW_SET)], row_send.at[0])
+    finish(near_rows, row_send.at[1])
+    for store in stores:
+        store.wait()
+
+
+def short_move(routes, queries, keys, values, own_rows):
+    lines, columns = keys.shape
+    kind = keys.dtype
+    chunks = 2 * PARTS
+    sizes = [room_size(room) for room in ROOM]
+    anywhere = pl.BlockSpec(memory_space=pltpu.HBM)
+
+    def vmem(*shape):
+        return pltpu.VMEM(shape, kind)
+
+    piece = (PIECE, LANES)
+    scratch = []
+    for count in (HELD, *sizes):
+        scratch += [vmem(count, *piece)] * chunks
+    scratch += [vmem(2, count, *piece) for count in (*sizes, HELD)]
+    scratch += [
+        vmem(2, HEADS, 2, BLOCK, LANES),
+        vmem(HEADS, BLOCK, 2 * BLOCK),
+        vmem(HEADS, HALF, 2 * BLOCK),
+        vmem(lines, columns),
+    ]
+    scratch += [vmem(BLOCK, columns)] * 4 + [vmem(lines, columns)]
+    scratch += [pltpu.VMEM((2 * HEADS, 2 * BLOCK), jnp.float32)]
+    scratch += [pltpu.SemaphoreType.DMA((2,))] * 2
+    scratch += [pltpu.SemaphoreType.DMA((3,))]
+    scratch += [pltpu.SemaphoreType.DMA((2,))] * 3
+    scratch += [pltpu.SemaphoreType.DMA((chunks,))] * 9
+    return pl.pallas_call(
+        short_kernel,
+        in_specs=[pl.BlockSpec(memory_space=pltpu.SMEM)] * 3
+        + [anywhere] * 3
+        + [pl.BlockSpec(memory_space=pltpu.VMEM)],
+        out_specs=anywhere,
+        out_shape=jax.ShapeDtypeStruct((lines, columns), kind),
+        scratch_shapes=scratch,
+        compiler_params=pltpu.CompilerParams(
+            collective_id=1, has_side_effects=True, vmem_limit_bytes=60 * 1024 * 1024
+        ),
+        name="short_move",
+    )(*routes, queries, keys, values, own_rows)
+
+
 def tile_table(partner):
     trio = partner // 3
     member = partner - 3 * trio
@@ -492,8 +1024,14 @@
     own_rows = jnp.einsum("skb,bh->hsk", one_hot, bias_table, precision=lax.Precision.HIGHEST)
     own_rows = jnp.pad(own_rows * math.log2(math.e), ((0, 0), (0, 0), (0, 1)))
 
-    return move_tiles(
-        tile_table(partner), queries, key_states, value_states, own_rows.reshape(ROW_SET, 2 * BLOCK)
+    own_rows = own_rows.reshape(ROW_SET, 2 * BLOCK)
+    *routes, over = plan_routes(partner)
+    return lax.cond(
+        over[0, 0] == 0,
+        lambda: short_move(routes, queries, key_states, value_states, own_rows),
+        lambda: move_tiles(
+            tile_table(partner), queries, key_states, value_states, own_rows
+        ),
     )
 
 

time: 295 us -> 283 us (0.959)
  Pallas kernels: 288 us -> 276 us
    pallas_call x1 -> x2, Pallas kernels: 288 us -> 276 us  [the longest x1 273 us: short_move(): pl.pallas_call(short_kernel, in_specs=[pl.BlockSpec(memory_space=pltpu.SM...]
where the time goes in v6:
time: 283 us; the launch traced here: 282 us
  Pallas kernels  276 us (98%)
  local copies, waits for them, and re-layouts  4.75 us (2%)
    pallas_call x1, Pallas kernels, short_move(): pl.pallas_call(short_kernel, in_specs=[pl.BlockSpec(memory_space=pltpu.SM...  273 us

profile of v6, /device:TPU:1, one launch (start us, length us, event | category | flops | bytes accessed | tf_op | source)
XLA Modules:
  0.0 282.5 jit_solution(3551157789774513813)
XLA Ops:
  0.0 0.0 copy-start
  0.0 0.7 copy-done
  0.7 0.8 fusion.26
  1.6 0.8 reshape.11
  2.4 0.7 reshape_reshape.6.row_ref
  3.2 0.8 reshape_reshape.8.column_ref
  4.0 2.9 %plan_routes.1 = (s32[1,368]{1,0:T(1,128)S(1)}, s32[1,400]{1,0:T(1,128)S(1)}, s32[1,384]{1,0:T(1,128)S(1)}, s32[1,1]{1,0:T(1,128)}) custom-call(s32[1,384]{1,0:T(1,128)} %reshape_reshape.6.row_ref, s32[384,1]{1,0:T(8,128)} %reshape_reshape.8.column_ref), custom_call_target="tpu_custom_call" | custom-call | tf_op jit(solution)/shard_map/plan_routes/pallas_call | solution.py:567
  7.6 273.2 %conditional.1 = (bf16[384,4096]{1,0:T(8,128)(2,1)S(1)}) conditional(s32[]{:T(128)} %bitcast.1, (s32[384]{0:T(512)}, bf16[384,4096]{1,0:T(8,128)(2,1)}, bf16[384,4096]{1,0:T(8,128)(2,1)}, bf16[384,4096]{1,0:T(8,128)(2,1)}, f32[8,512]{1,0:T(8,128)S(1)}) %tuple.11, (s32[1,368]{1,0:T(1,128)S(1)}, s32[1,400]{1,0:T(1,128)S(1)}, s32[1,384]{1,0:T(1,128)S(1)}, ...), branch_computations={%region_0.1_spmd, %region_1.2_spmd} | conditional | flops 58368 | bytes 1073752576 | solution.py:1029
  7.6 273.0 %short_move.1 = bf16[384,4096]{1,0:T(8,128)(2,1)S(1)} custom-call(s32[1,368]{1,0:T(1,128)S(1)} %get-tuple-element.37.send_ref, s32[1,400]{1,0:T(1,128)S(1)} %get-tuple-element.38.relay_ref, s32[1,384]{1,0:T(1,128)S(1)} %get-tuple-element.39.final_ref, bf16[384,4096]{1,0:T(8,128)(2,1)} %get-tuple-element.40.q_ref, bf16[384,4096]{1,0:T(8,128)(2,1)} %get-tuple-element.41.k_ref, ...), custom_call_target="tpu_custom_call" | custom-call | tf_op jit(solution)/shard_map/cond/branch_1_fun/short_move/pallas_call | solution.py:989
  280.8 1.7 copy.17
  (4 shorter events, 0.0 us)
Async XLA Ops:
  0.0 0.7 copy-start

commit v7 on v6

--- a/solution.py
+++ b/solution.py
@@ -470,10 +470,16 @@
 
 
 PARTS = 4
-PIECE = BLOCK // PARTS
+SPANS = (((0, 32), (32, 96), (128, 64), (192, 64)), ((0, 64), (64, 64), (128, 96), (224, 32)))
 HELD = 48
-ROOM = ((13, 10), (14, 11))
+ROOM = ((13, 10), (12, 11))
+FLIP = (11, 12)
 HOPS = (2, 1, -1, -2)
+
+
+def span_of(chunk):
+    kind, part = divmod(chunk, PARTS)
+    return kind, *SPANS[kind][part]
 
 
 def room_starts(room):
@@ -485,47 +491,74 @@
     return 2 * sum(room)
 
 
-def route_kernel(row_ref, column_ref, send_ref, relay_ref, final_ref, over_ref):
-    count = row_ref.shape[1]
+def route_kernel(partner_ref, send_ref, relay_ref, final_ref, over_ref):
+    count = partner_ref.shape[1]
     i_row = lax.broadcasted_iota(jnp.int32, (1, count), 1)
     i_column = lax.broadcasted_iota(jnp.int32, (count, 1), 0)
 
     def both(f, *pairs):
         return tuple(f(*(pair[s] for pair in pairs)) for s in range(2))
 
-    def rank(key):
+    i = (i_row, i_column)
+
+    def rank(key, order=i):
         same = key[1] == key[0]
-        in_row = jnp.sum(jnp.where(same & (i_column < i_row), 1.0, 0.0), axis=0, keepdims=True)
-        in_column = jnp.sum(jnp.where(same & (i_row < i_column), 1.0, 0.0), axis=1, keepdims=True)
+        before = jnp.where(same & (order[1] < order[0]), 1.0, 0.0)
+        after = jnp.where(same & (order[0] < order[1]), 1.0, 0.0)
+        in_row = jnp.sum(before, axis=0, keepdims=True)
+        in_column = jnp.sum(after, axis=1, keepdims=True)
         return in_row.astype(jnp.int32), in_column.astype(jnp.int32)
 
-    block = (row_ref[...], column_ref[...])
+    asked = partner_ref[...].astype(jnp.float32)
+    in_plane = i_column - HELD * (i_column // HELD)
+    group = in_plane // 6
+    wanted = ((i_column // 96) * 8 + group) * 12 + in_plane - 6 * group
+    wanted = wanted + jnp.where(i_column - 96 * (i_column // 96) >= HELD, 6, 0)
+    block_column = jnp.sum(jnp.where(wanted == i_row, asked, 0.0), axis=1, keepdims=True)
+    block_row = jnp.sum(jnp.where(i_column == i_row, block_column, 0.0), axis=0, keepdims=True)
+    block = (block_row.astype(jnp.int32), block_column.astype(jnp.int32))
     seq = both(lambda m: m // 12, block)
     rest = both(lambda m, s: m - 12 * s, block, seq)
     source = both(lambda s, r: (s // 8) * 2 + jnp.where(r >= 6, 1, 0), seq, rest)
     local = both(
         lambda s, r: (s - 8 * (s // 8)) * 6 + jnp.where(r >= 6, r - 6, r), seq, rest
     )
-    target = both(lambda i: i // HELD, (i_row, i_column))
+    target = both(lambda i: i // HELD, i)
     ahead = both(lambda a, b: jnp.where(b >= a, b - a, b - a + PLANES), source, target)
     turn = both(lambda r: r - 2 * (r // 2), rank(both(lambda a, b: a * 8 + b, source, target)))
     sign = both(
         lambda k, t: jnp.where(k < 4, 1, jnp.where((k == 4) & (t == 0), 1, -1)), ahead, turn
     )
     distance = both(lambda k: jnp.where(k <= 4, k, PLANES - k), ahead)
-    first = both(
-        lambda d, t: jnp.where(
-            d == 0,
-            0,
-            jnp.where(d == 1, t, jnp.where(d == 2, 2 * t, jnp.where(d == 3, 1 + t, 2))),
-        ),
-        distance,
-        turn,
-    )
-    second = both(lambda d, o: d - o, distance, first)
-    relay = both(
-        lambda z, s, o: jnp.bitwise_and(z + s * o + PLANES, PLANES - 1), source, sign, first
-    )
+    def split(turn):
+        first = both(
+            lambda d, t: jnp.where(
+                d == 0,
+                0,
+                jnp.where(d == 1, t, jnp.where(d == 2, 2 * t, jnp.where(d == 3, 1 + t, 2))),
+            ),
+            distance,
+            turn,
+        )
+        second = both(lambda d, o: d - o, distance, first)
+        relay = both(
+            lambda z, s, o: jnp.bitwise_and(z + s * o + PLANES, PLANES - 1), source, sign, first
+        )
+        return first, second, relay
+
+    late = both(lambda d, i: jnp.where(d == 4, i, i + count), distance, i)
+    for leg in range(2):
+        first, second, relay = split(turn)
+        plane, hop = ((source, first), (relay, second))[leg]
+        crowd = rank(both(lambda p, s, h: p * 8 + s * h + 2, plane, sign, hop), late)
+        turn = both(
+            lambda t, d, h, r: jnp.where((h == 2) & (d < 4) & (r >= FLIP[leg]), leg, t),
+            turn,
+            distance,
+            hop,
+            crowd,
+        )
+    first, second, relay = split(turn)
 
     def slots(plane, hop, room):
         way = both(lambda s, h: jnp.where(h == 0, 0, s * h), sign, hop)
@@ -561,16 +594,16 @@
 
 
 def plan_routes(partner):
-    order = partner.reshape(4, 8, 2, 6).transpose(0, 2, 1, 3).reshape(-1)
     full = pl.BlockSpec(memory_space=pltpu.VMEM)
-    shapes = [(1, PLANES * room_size(room)) for room in ROOM] + [(1, order.shape[0]), (1, 1)]
+    count = partner.shape[0]
+    shapes = [(1, PLANES * room_size(room)) for room in ROOM] + [(1, count), (1, 1)]
     return pl.pallas_call(
         route_kernel,
-        in_specs=[full] * 2,
+        in_specs=[full],
         out_specs=[full] * 4,
         out_shape=[jax.ShapeDtypeStruct(shape, jnp.int32) for shape in shapes],
         name="plan_routes",
-    )(order.reshape(1, -1), order.reshape(-1, 1))
+    )(partner.reshape(1, -1))
 
 
 def short_kernel(
@@ -662,35 +695,38 @@
     half_rows = pl.ds(pl.multiple_of(2 * HALF * (1 - odd), HALF), HALF)
 
     def spread(chunk):
-        kind, part = divmod(chunk, PARTS)
+        kind, start, size = span_of(chunk)
         ref = (k_ref, v_ref)[kind]
 
-        def piece(start):
-            lines = pl.ds(pl.multiple_of(start, PIECE), PIECE)
+        def piece(base):
+            lines = pl.ds(pl.multiple_of(base, 2 * ROWS), size)
             return lambda other: ref.at[
                 lines, pl.ds(pl.multiple_of(other * LANES, LANES), LANES)
             ]
 
         plane_stage(
-            piece(odd * HALF + PIECE * part),
+            piece(odd * HALF + start),
             held[chunk].at[first_block(spot) + 2 * odd],
             p0_send.at[chunk],
             p0_recv.at[chunk],
         )
 
-        @pl.when(odd == part // 2)
+        @pl.when(odd == start // HALF)
         def _():
             plane_stage(
-                piece(2 * HALF * (1 - odd) + PIECE * (part % 2)),
+                piece(2 * HALF * (1 - odd) + start % HALF),
                 held[chunk].at[first_block(spot) + 1],
                 p0b_send.at[chunk],
                 p0_recv.at[chunk],
             )
 
-    def z_stage(staged, landed, room, send, recv):
+    def staged(ref, chunk):
+        return ref.at[chunk % 2, :, pl.ds(0, span_of(chunk)[2])]
+
+    def z_stage(source, landed, room, send, recv):
         for start, size, hop in zip(room_starts(room), (*room, *room[::-1]), HOPS):
             pltpu.make_async_remote_copy(
-                src_ref=staged.at[pl.ds(start, size)],
+                src_ref=source.at[pl.ds(start, size)],
                 dst_ref=landed.at[pl.ds(start, size)],
                 send_sem=send,
                 recv_sem=recv,
@@ -702,18 +738,21 @@
 
     def leg_one(chunk):
         finish(held[chunk], p0_recv.at[chunk])
-        slot = chunk % 2
+        slot, size = chunk % 2, span_of(chunk)[2]
         if chunk >= 2:
-            finish(staged_one.at[slot], z1_send.at[chunk - 2])
+            finish(staged(staged_one, chunk - 2), z1_send.at[chunk - 2])
 
         def body(i, carry):
             for j in range(2):
                 where = 2 * i + j
-                staged_one[slot, where] = held[chunk][send_ref[0, plane * size_one + where]]
+                index = send_ref[0, plane * size_one + where]
+                staged_one[slot, where, :size] = held[chunk][index]
             return carry
 
         lax.fori_loop(0, size_one // 2, body, 0)
-        z_stage(staged_one.at[slot], near_in[chunk], ROOM[0], z1_send.at[chunk], z1_recv.at[chunk])
+        z_stage(
+            staged(staged_one, chunk), near_in[chunk], ROOM[0], z1_send.at[chunk], z1_recv.at[chunk]
+        )
 
     def held_or_near(chunk, index):
         kept = held[chunk][jnp.minimum(index, HELD - 1)]
@@ -722,23 +761,25 @@
 
     def leg_two(chunk):
         finish(near_in[chunk], z1_recv.at[chunk])
-        slot = chunk % 2
+        slot, size = chunk % 2, span_of(chunk)[2]
         if chunk >= 2:
-            finish(staged_two.at[slot], z2_send.at[chunk - 2])
+            finish(staged(staged_two, chunk - 2), z2_send.at[chunk - 2])
 
         def body(i, carry):
             for j in range(2):
                 where = 2 * i + j
                 index = relay_ref[0, plane * size_two + where]
-                staged_two[slot, where] = held_or_near(chunk, index)
+                staged_two[slot, where, :size] = held_or_near(chunk, index)
             return carry
 
         lax.fori_loop(0, size_two // 2, body, 0)
-        z_stage(staged_two.at[slot], far_in[chunk], ROOM[1], z2_send.at[chunk], z2_recv.at[chunk])
+        z_stage(
+            staged(staged_two, chunk), far_in[chunk], ROOM[1], z2_send.at[chunk], z2_recv.at[chunk]
+        )
 
     def arrived(chunk, count=PLANE_DEVICES):
-        kind, part = divmod(chunk, PARTS)
-        return far_ref.at[kind, pl.ds(0, count), :, pl.ds(part * PIECE, PIECE)]
+        kind, start, size = span_of(chunk)
+        return far_ref.at[kind, pl.ds(0, count), :, pl.ds(start, size)]
 
     done = set()
 
@@ -749,7 +790,7 @@
 
     def deliver(chunk):
         finish(far_in[chunk], z2_recv.at[chunk])
-        slot = chunk % 2
+        slot, (kind, start, size) = chunk % 2, span_of(chunk)
         if chunk >= 2:
             finish(arrived(chunk - 2, PLANE_DEVICES - 1), out_send.at[chunk - 2])
             finish_far(chunk - 2)
@@ -760,16 +801,16 @@
                 where = 2 * i + j
                 index = final_ref[0, plane * HELD + where]
                 last = far_in[chunk][jnp.clip(index - border, 0, size_two - 1)]
-                staged_out[slot, where] = jnp.where(
+                staged_out[slot, where, :size] = jnp.where(
                     index < border, held_or_near(chunk, index), last
                 )
             return carry
 
         lax.fori_loop(0, HELD // 2, body, 0)
-        kind, part = divmod(chunk, PARTS)
+        ready = staged(staged_out, chunk)
         plane_stage(
-            lambda other: staged_out.at[slot, pl.ds(first_block(other) + lax.rem(other, 2), 2)],
-            far_ref.at[kind, spot, :, pl.ds(part * PIECE, PIECE)],
+            lambda other: ready.at[pl.ds(first_block(other) + lax.rem(other, 2), 2)],
+            far_ref.at[kind, spot, :, pl.ds(start, size)],
             out_send.at[chunk],
             out_recv.at[chunk],
         )
@@ -943,13 +984,13 @@
     for chunk in range(chunks):
         finish(arrived(chunk, PLANE_DEVICES - 1).at[:, 0], p0_send.at[chunk])
 
-        @pl.when(odd == chunk % PARTS // 2)
+        @pl.when(odd == span_of(chunk)[1] // HALF)
         def _():
             finish(arrived(chunk, PLANE_DEVICES - 1).at[:, 0], p0b_send.at[chunk])
 
     for chunk in range(chunks - 2, chunks):
-        finish(staged_one.at[chunk % 2], z1_send.at[chunk])
-        finish(staged_two.at[chunk % 2], z2_send.at[chunk])
+        finish(staged(staged_one, chunk), z1_send.at[chunk])
+        finish(staged(staged_two, chunk), z2_send.at[chunk])
         finish(arrived(chunk, PLANE_DEVICES - 1), out_send.at[chunk])
     for i, target in enumerate((mid_k, mid_v)):
         finish(target.at[pl.ds(0, HALF), :], half_send.at[i])
@@ -969,11 +1010,11 @@
     def vmem(*shape):
         return pltpu.VMEM(shape, kind)
 
-    piece = (PIECE, LANES)
+    spans = [span_of(chunk)[2] for chunk in range(chunks)]
     scratch = []
     for count in (HELD, *sizes):
-        scratch += [vmem(count, *piece)] * chunks
-    scratch += [vmem(2, count, *piece) for count in (*sizes, HELD)]
+        scratch += [vmem(count, size, LANES) for size in spans]
+    scratch += [vmem(2, count, max(spans), LANES) for count in (*sizes, HELD)]
     scratch += [
         vmem(2, HEADS, 2, BLOCK, LANES),
         vmem(HEADS, BLOCK, 2 * BLOCK),

time: 283 us -> 281 us (level)
  no operation moved by 1% of the time
where the time goes in v7:
time: 281 us
  Pallas kernels  276 us (98%)
  local copies, waits for them, and re-layouts  2.96 us (1%)
    pallas_call x1, Pallas kernels, short_move(): pl.pallas_call(short_kernel, in_specs=[pl.BlockSpec(memory_space=pltpu.SM...  272 us

profile of v7, /device:TPU:1, one launch (start us, length us, event | category | flops | bytes accessed | tf_op | source)
XLA Modules:
  0.0 280.7 jit_solution(13920290490880743588)
XLA Ops:
  0.0 0.0 copy-start
  0.0 1.3 reshape.11.partner_ref
  1.3 3.6 %plan_routes.1 = (s32[1,368]{1,0:T(1,128)S(1)}, s32[1,368]{1,0:T(1,128)S(1)}, s32[1,384]{1,0:T(1,128)S(1)}, s32[1,1]{1,0:T(1,128)}) custom-call(s32[1,384]{1,0:T(1,128)} %reshape.11.partner_ref), custom_call_target="tpu_custom_call" | custom-call | tf_op jit(solution)/shard_map/plan_routes/pallas_call | solution.py:600
  5.5 0.0 copy-done
  5.5 0.8 fusion.26
  6.4 272.6 %conditional.1 = (bf16[384,4096]{1,0:T(8,128)(2,1)S(1)}) conditional(s32[]{:T(128)} %bitcast, (s32[384]{0:T(512)}, bf16[384,4096]{1,0:T(8,128)(2,1)}, bf16[384,4096]{1,0:T(8,128)(2,1)}, bf16[384,4096]{1,0:T(8,128)(2,1)}, f32[8,512]{1,0:T(8,128)S(1)}) %tuple.11, (s32[1,368]{1,0:T(1,128)S(1)}, s32[1,368]{1,0:T(1,128)S(1)}, s32[1,384]{1,0:T(1,128)S(1)}, ...), branch_computations={%region_0.1_spmd, %region_1.2_spmd} | conditional | flops 58368 | bytes 1073752576 | solution.py:1070
  6.4 272.4 %short_move.1 = bf16[384,4096]{1,0:T(8,128)(2,1)S(1)} custom-call(s32[1,368]{1,0:T(1,128)S(1)} %get-tuple-element.37.send_ref, s32[1,368]{1,0:T(1,128)S(1)} %get-tuple-element.38.relay_ref, s32[1,384]{1,0:T(1,128)S(1)} %get-tuple-element.39.final_ref, bf16[384,4096]{1,0:T(8,128)(2,1)} %get-tuple-element.40.q_ref, bf16[384,4096]{1,0:T(8,128)(2,1)} %get-tuple-element.41.k_ref, ...), custom_call_target="tpu_custom_call" | custom-call | tf_op jit(solution)/shard_map/cond/branch_1_fun/short_move/pallas_call | solution.py:1030
  279.0 1.7 copy.14
  (3 shorter events, 0.0 us)
Async XLA Ops:
  0.0 5.5 %copy-start = (f32[32,4]{0,1:T(4,128)S(1)}, f32[32,4]{0,1:T(4,128)}, u32[]{:S(2)}) copy-start(f32[32,4]{0,1:T(4,128)} %param.13) | copy-start | bytes 1540

commit v8 on v7

--- a/solution.py
+++ b/solution.py
@@ -947,7 +947,7 @@
     show_rows()
     for load in loads:
         load.start()
-    for step in range(chunks + 2):
+    for step in range(chunks + 3):
         if step < chunks:
             leg_one(step)
             if step + 2 < chunks:
@@ -955,11 +955,11 @@
         if step == 1:
             share_rows()
             swap_halves()
-        if 1 <= step <= chunks:
+        if 1 <= step < chunks + 1:
             leg_two(step - 1)
-        if step >= 2:
-            deliver(step - 2)
-        turn = step - chunks + 2
+        if step >= 3:
+            deliver(step - 3)
+        turn = step - chunks + 1
         if turn == 0:
             for chunk in range(PARTS):
                 finish_far(chunk)

time: 281 us -> 271 us (0.964)
  Pallas kernels: 276 us -> 266 us
    pallas_call x1, Pallas kernels: 272 us -> 263 us  [short_move(): pl.pallas_call(short_kernel, in_specs=[pl.BlockSpec(memory_space=pltpu.SM...]
where the time goes in v8:
time: 271 us
  Pallas kernels  266 us (98%)
  local copies, waits for them, and re-layouts  2.96 us (1%)
    pallas_call x1, Pallas kernels, short_move(): pl.pallas_call(short_kernel, in_specs=[pl.BlockSpec(memory_space=pltpu.SM...  263 us

profile of v8, /device:TPU:1, one launch (start us, length us, event | category | flops | bytes accessed | tf_op | source)
XLA Modules:
  0.0 270.9 jit_solution(12869807651729921917)
XLA Ops:
  0.0 0.0 copy-start
  0.0 1.3 reshape.11.partner_ref
  1.3 3.6 %plan_routes.1 = (s32[1,368]{1,0:T(1,128)S(1)}, s32[1,368]{1,0:T(1,128)S(1)}, s32[1,384]{1,0:T(1,128)S(1)}, s32[1,1]{1,0:T(1,128)}) custom-call(s32[1,384]{1,0:T(1,128)} %reshape.11.partner_ref), custom_call_target="tpu_custom_call" | custom-call | tf_op jit(solution)/shard_map/plan_routes/pallas_call | solution.py:600
  5.5 0.0 copy-done
  5.5 0.8 fusion.26
  6.4 262.9 %conditional.1 = (bf16[384,4096]{1,0:T(8,128)(2,1)S(1)}) conditional(s32[]{:T(128)} %bitcast, (s32[384]{0:T(512)}, bf16[384,4096]{1,0:T(8,128)(2,1)}, bf16[384,4096]{1,0:T(8,128)(2,1)}, bf16[384,4096]{1,0:T(8,128)(2,1)}, f32[8,512]{1,0:T(8,128)S(1)}) %tuple.11, (s32[1,368]{1,0:T(1,128)S(1)}, s32[1,368]{1,0:T(1,128)S(1)}, s32[1,384]{1,0:T(1,128)S(1)}, ...), branch_computations={%region_0.1_spmd, %region_1.2_spmd} | conditional | flops 58368 | bytes 1073752576 | solution.py:1070
  6.4 262.6 %short_move.1 = bf16[384,4096]{1,0:T(8,128)(2,1)S(1)} custom-call(s32[1,368]{1,0:T(1,128)S(1)} %get-tuple-element.37.send_ref, s32[1,368]{1,0:T(1,128)S(1)} %get-tuple-element.38.relay_ref, s32[1,384]{1,0:T(1,128)S(1)} %get-tuple-element.39.final_ref, bf16[384,4096]{1,0:T(8,128)(2,1)} %get-tuple-element.40.q_ref, bf16[384,4096]{1,0:T(8,128)(2,1)} %get-tuple-element.41.k_ref, ...), custom_call_target="tpu_custom_call" | custom-call | tf_op jit(solution)/shard_map/cond/branch_1_fun/short_move/pallas_call | solution.py:1030
  269.3 1.7 copy.14
  (3 shorter events, 0.0 us)
Async XLA Ops:
  0.0 5.5 %copy-start = (f32[32,4]{0,1:T(4,128)S(1)}, f32[32,4]{0,1:T(4,128)}, u32[]{:S(2)}) copy-start(f32[32,4]{0,1:T(4,128)} %param.13) | copy-start | bytes 1540

commit v9 on v8

--- a/solution.py
+++ b/solution.py
@@ -470,7 +470,7 @@
 
 
 PARTS = 4
-SPANS = (((0, 32), (32, 96), (128, 64), (192, 64)), ((0, 64), (64, 64), (128, 96), (224, 32)))
+SPANS = (((0, 64), (64, 64), (128, 64), (192, 64)), ((0, 64), (64, 64), (128, 64), (192, 64)))
 HELD = 48
 ROOM = ((13, 10), (12, 11))
 FLIP = (11, 12)

time: 271 us -> 266 us (0.982)
  Pallas kernels: 266 us -> 261 us
    pallas_call x1, Pallas kernels: 263 us -> 257 us  [short_move(): pl.pallas_call(short_kernel, in_specs=[pl.BlockSpec(memory_space=pltpu.SM...]
where the time goes in v9:
time: 266 us
  Pallas kernels  261 us (98%)
  local copies, waits for them, and re-layouts  2.96 us (1%)
    pallas_call x1, Pallas kernels, short_move(): pl.pallas_call(short_kernel, in_specs=[pl.BlockSpec(memory_space=pltpu.SM...  257 us

profile of v9, /device:TPU:1, one launch (start us, length us, event | category | flops | bytes accessed | tf_op | source)
XLA Modules:
  0.0 265.8 jit_solution(7067856953593533404)
XLA Ops:
  0.0 0.0 copy-start
  0.0 1.3 reshape.11.partner_ref
  1.3 3.6 %plan_routes.1 = (s32[1,368]{1,0:T(1,128)S(1)}, s32[1,368]{1,0:T(1,128)S(1)}, s32[1,384]{1,0:T(1,128)S(1)}, s32[1,1]{1,0:T(1,128)}) custom-call(s32[1,384]{1,0:T(1,128)} %reshape.11.partner_ref), custom_call_target="tpu_custom_call" | custom-call | tf_op jit(solution)/shard_map/plan_routes/pallas_call | solution.py:600
  5.5 0.0 copy-done
  5.5 0.8 fusion.26
  6.4 257.7 %conditional.1 = (bf16[384,4096]{1,0:T(8,128)(2,1)S(1)}) conditional(s32[]{:T(128)} %bitcast, (s32[384]{0:T(512)}, bf16[384,4096]{1,0:T(8,128)(2,1)}, bf16[384,4096]{1,0:T(8,128)(2,1)}, bf16[384,4096]{1,0:T(8,128)(2,1)}, f32[8,512]{1,0:T(8,128)S(1)}) %tuple.11, (s32[1,368]{1,0:T(1,128)S(1)}, s32[1,368]{1,0:T(1,128)S(1)}, s32[1,384]{1,0:T(1,128)S(1)}, ...), branch_computations={%region_0.1_spmd, %region_1.2_spmd} | conditional | flops 58368 | bytes 1073752576 | solution.py:1070
  6.4 257.5 %short_move.1 = bf16[384,4096]{1,0:T(8,128)(2,1)S(1)} custom-call(s32[1,368]{1,0:T(1,128)S(1)} %get-tuple-element.37.send_ref, s32[1,368]{1,0:T(1,128)S(1)} %get-tuple-element.38.relay_ref, s32[1,384]{1,0:T(1,128)S(1)} %get-tuple-element.39.final_ref, bf16[384,4096]{1,0:T(8,128)(2,1)} %get-tuple-element.40.q_ref, bf16[384,4096]{1,0:T(8,128)(2,1)} %get-tuple-element.41.k_ref, ...), custom_call_target="tpu_custom_call" | custom-call | tf_op jit(solution)/shard_map/cond/branch_1_fun/short_move/pallas_call | solution.py:1030
  264.1 1.7 copy.14
  (3 shorter events, 0.0 us)
Async XLA Ops:
  0.0 5.5 %copy-start = (f32[32,4]{0,1:T(4,128)S(1)}, f32[32,4]{0,1:T(4,128)}, u32[]{:S(2)}) copy-start(f32[32,4]{0,1:T(4,128)} %param.13) | copy-start | bytes 1540
